TPU v7x, 1024 devices: a whole 4x4x32 slice. The times are simulated.
1024 devices in a mesh: dp: 8 (over y, core), ctx: 16 (over z_hi, x), tp: 8 (over z_lo).
Axes of the slice: x: 4, y: 4, z: 32 (z_hi: 4, z_lo: 8; z = z_hi * 8 + z_lo), core: 2. Of those that a mesh axis runs over, the one named last changes fastest.
Arguments:
- queries: bfloat16 [128, 512, 4096], P(('dp', 'ctx'), None, 'tp'), may hold values from -400 to 400
- key_rows: bfloat16 [128, 512, 1024], P(('dp', 'ctx'), None, 'tp'), may hold values from -6 to 6
- value_rows: bfloat16 [128, 512, 1024], P(('dp', 'ctx'), None, 'tp'), may hold values from -6 to 6
- out_grad: bfloat16 [128, 512, 4096], P(('dp', 'ctx'), None, 'tp'), may hold values from -6 to 6
- inputs: bfloat16 [128, 512, 8192], P(('dp', 'ctx'), None, 'tp'), may hold values from -0.09375 to 0.09375
- doc_lengths: int32 [128, 16], P('dp'), may hold values from 1 to 40, 512 in all within a row
- doc_plan: int32 [128, 16], P('dp'), may hold values from 0 to 15, each once within a row
Outputs:
- query_grad: bfloat16 [128, 640, 4096], P(('dp', 'ctx'), None, 'tp')
- key_grad: bfloat16 [128, 640, 1024], P(('dp', 'ctx'), None, 'tp')
- value_grad: bfloat16 [128, 640, 1024], P(('dp', 'ctx'), None, 'tp')
- weight_grad: float32 [8192, 1024], P(('tp', 'dp', 'ctx'))
Inputs may be any that keep to these rules, and one draw needn't show every extreme that they name: `doc_lengths`: each row sums to 512; every document has at most 40 tokens, and one of each row has exactly 40. Each row is a permutation: document d of sequence s goes to context index doc_plan[s, d] of the same data group.
All inputs are finite; a program needn't handle non-finite values.
Results may differ from a plain program's by a relative error of at most 0.012.
Values may be sent and summed in bfloat16 or wider, within the bound.
No kernel may reach another device: no remote copies, remote signals or barrier semaphores. Data moves between devices by JAX's collectives and lax.ppermute only.
A program may use at most 32 MiB of HBM per device.

v0:
```python
import jax
import jax.numpy as jnp
from jax import lax
from jax.sharding import PartitionSpec as P

HEADS = 32
KVH = 8
HD = 128


def head_grads(query_part, key_part, value_part, grad_part, allowed):
    score_scale = HD ** (-0.5)
    scores = (
        jnp.einsum("nrch,nsch->ncrs", query_part, key_part, preferred_element_type=jnp.float32)
        * score_scale
    )
    scores = jnp.where(allowed[:, None, :, :], scores, -jnp.inf)
    largest = jnp.max(scores, axis=3, keepdims=True)
    raised = jnp.exp(scores - largest)
    weights = raised / jnp.sum(raised, axis=3, keepdims=True)
    weights_low = weights.astype(jnp.bfloat16)
    attended = jnp.einsum(
        "ncrs,nsch->nrch", weights_low, value_part, preferred_element_type=jnp.float32
    )
    row_delta = jnp.einsum("nrch,nrch->ncr", grad_part.astype(jnp.float32), attended)
    prob_grad = jnp.einsum(
        "nrch,nsch->ncrs", grad_part, value_part, preferred_element_type=jnp.float32
    )
    dscore = (weights * (prob_grad - row_delta[..., None])).astype(jnp.bfloat16)
    query_grad = (
        jnp.einsum("ncrs,nsch->nrch", dscore, key_part, preferred_element_type=jnp.float32)
        * score_scale
    )
    key_grad = (
        jnp.einsum("ncrs,nrch->nsch", dscore, query_part, preferred_element_type=jnp.float32)
        * score_scale
    )
    value_grad = jnp.einsum(
        "ncrs,nrch->nsch", weights_low, grad_part, preferred_element_type=jnp.float32
    )
    return (query_grad, key_grad, value_grad)


def attend_blocks(query_in, key_in, value_in, grad_in, live_rows):
    blocks, capacity = live_rows.shape
    received = blocks * capacity
    kv_local = key_in.shape[1] // HD
    group_size = HEADS // KVH
    offsets = jnp.arange(capacity, dtype=jnp.int32)
    self_pair = offsets[None, None, :] == offsets[None, :, None]
    allowed = (offsets[None, None, :] <= offsets[None, :, None]) & (
        live_rows[:, :, None] | self_pair
    )
    query_stack = jnp.moveaxis(query_in.reshape(blocks, capacity, kv_local, group_size, HD), 3, 0)
    grad_stack = jnp.moveaxis(grad_in.reshape(blocks, capacity, kv_local, group_size, HD), 3, 0)
    key_part = key_in.reshape(blocks, capacity, kv_local, HD)
    value_part = value_in.reshape(blocks, capacity, kv_local, HD)

    def one_head(members):
        return head_grads(members[0], key_part, value_part, members[1], allowed)

    head_q, head_k, head_v = jax.vmap(one_head)((query_stack, grad_stack))
    query_grad = (
        jnp.moveaxis(head_q, 0, 3)
        .reshape(received, kv_local * group_size * HD)
        .astype(jnp.bfloat16)
    )
    key_grad = jnp.sum(head_k, axis=0).reshape(received, kv_local * HD).astype(jnp.bfloat16)
    value_grad = jnp.sum(head_v, axis=0).reshape(received, kv_local * HD).astype(jnp.bfloat16)
    return (query_grad, key_grad, value_grad)


def shards(queries, key_rows, value_rows, out_grad, inputs, doc_lengths, doc_plan):
    n_ctx = lax.axis_size("ctx")
    own_index = lax.axis_index("ctx")
    seq_len = queries.shape[1]
    capacity = 5 * seq_len // (4 * n_ctx)
    received = n_ctx * capacity
    starts = jnp.cumsum(doc_lengths, axis=1) - doc_lengths
    doc_ids = jnp.arange(n_ctx, dtype=jnp.int32)
    matches = (doc_plan[:, None, :] == doc_ids[None, :, None]).astype(jnp.int32)
    inverse = jnp.sum(doc_ids[None, None, :] * matches, axis=2)
    offsets = jnp.arange(capacity, dtype=jnp.int32)
    own_lengths = lax.dynamic_index_in_dim(doc_lengths, own_index, 0, keepdims=False)
    own_starts = lax.dynamic_index_in_dim(starts, own_index, 0, keepdims=False)
    outgoing = lax.dynamic_index_in_dim(inverse, own_index, 0, keepdims=False)
    send_len = jnp.take(own_lengths, outgoing)
    send_first = jnp.take(own_starts, outgoing)
    send_live = offsets[None, :] < send_len[:, None]
    send_valid = send_live.reshape(received, 1)
    send_pos = jnp.minimum(send_first[:, None] + offsets[None, :], seq_len - 1).reshape(received)

    def pack_rows(source):
        picked = jnp.take(source[0], send_pos, axis=0)
        return jnp.where(send_valid, picked, jnp.zeros((), source.dtype))

    query_in, key_in, value_in, grad_in = (
        lax.all_to_all(pack_rows(queries), "ctx", split_axis=0, concat_axis=0, tiled=True),
        lax.all_to_all(pack_rows(key_rows), "ctx", split_axis=0, concat_axis=0, tiled=True),
        lax.all_to_all(pack_rows(value_rows), "ctx", split_axis=0, concat_axis=0, tiled=True),
        lax.all_to_all(pack_rows(out_grad), "ctx", split_axis=0, concat_axis=0, tiled=True),
    )
    incoming = lax.dynamic_index_in_dim(inverse, own_index, 1, keepdims=False)
    recv_len = jnp.sum(jnp.where(doc_ids[None, :] == incoming[:, None], doc_lengths, 0), axis=1)
    recv_live = offsets[None, :] < recv_len[:, None]
    query_grad, key_grad, value_grad = attend_blocks(query_in, key_in, value_in, grad_in, recv_live)
    input_rows = lax.all_to_all(pack_rows(inputs), "ctx", split_axis=0, concat_axis=0, tiled=True)
    partial_term = jnp.einsum(
        "ra,rc->ac",
        input_rows,
        lax.all_gather(value_grad, "tp", axis=1, tiled=True),
        preferred_element_type=jnp.float32,
    )
    weight_grad = lax.psum_scatter(partial_term, ("dp", "ctx"), scatter_dimension=0, tiled=True)
    return (query_grad[None], key_grad[None], value_grad[None], weight_grad)


def solution(mesh):
    placed = (
        P(("dp", "ctx"), None, "tp"),
        P(("dp", "ctx"), None, "tp"),
        P(("dp", "ctx"), None, "tp"),
        P(("dp", "ctx"), None, "tp"),
        P(("dp", "ctx"), None, "tp"),
        P("dp", None),
        P("dp", None),
    )
    return jax.shard_map(
        shards,
        mesh=mesh,
        in_specs=placed,
        out_specs=(
            P(("dp", "ctx"), None, "tp"),
            P(("dp", "ctx"), None, "tp"),
            P(("dp", "ctx"), None, "tp"),
            P(("tp", "dp", "ctx"), None),
        ),
        check_vma=False,
    )
```

profile of v0, /device:TPU:224, one launch (start us, length us, event | category | flops | bytes accessed | tf_op | source)
XLA Modules:
  0.0 1534.9 jit_solution(8695256642515573510)
XLA Ops:
  7.2 1.2 select_reduce_fusion
  11.7 2.0 gather_fusion.6
  13.7 2.0 gather_fusion.3
  16.7 23.4 %all-to-all-start = ((bf16[16,40,128]{2,1,0:T(8,128)(2,1)}), bf16[16,40,128]{2,1,0:T(8,128)(2,1)S(1)}, u32[]{:S(2)}, u32[]{:S(2)}) async-start(bf16[16,40,128]{2,1,0:T(8,128)(2,1)} %bitcast.4), calls=%async_computation | async-start | bytes 327680 | tf_op jit(solution)/shard_map/all_to_all | solution.py:99
  40.1 2.8 gather_fusion.5
  42.9 2.8 gather_fusion.4
  45.7 1.1 select_select_fusion.1
  46.8 24.2 %all-to-all-done = bf16[16,40,128]{2,1,0:T(8,128)(2,1)S(1)} async-done(((bf16[16,40,128]{2,1,0:T(8,128)(2,1)}), bf16[16,40,128]{2,1,0:T(8,128)(2,1)S(1)}, u32[]{:S(2)}, u32[]{:S(2)}) %all-to-all-start) | async-done | bytes 163872 | tf_op jit(solution)/shard_map/all_to_all | solution.py:99
  71.1 48.4 %all_to_all.45 = bf16[16,40,512]{2,1,0:T(8,128)(2,1)S(1)} all-to-all(bf16[16,40,512]{2,1,0:T(8,128)(2,1)S(1)} %bitcast.132), channel_id=1, replica_groups=mesh['dp'=8,'ctx'=16,'tp'=8] {'ctx'}, dimensions={0} | all-to-all | bytes 1310720 | tf_op jit(solution)/shard_map/all_to_all | solution.py:98
  119.4 35.5 %all-to-all-start.2 = ((bf16[16,40,512]{2,1,0:T(8,128)(2,1)}), bf16[16,40,512]{2,1,0:T(8,128)(2,1)}, u32[]{:S(2)}, u32[]{:S(2)}) async-start(bf16[16,40,512]{2,1,0:T(8,128)(2,1)} %bitcast.15), calls=%async_computation.2 | async-start | bytes 1310720 | tf_op jit(solution)/shard_map/all_to_all | solution.py:101
  155.1 2.8 gather_fusion
  157.9 1.3 select_select_fusion
  159.2 23.7 %all-to-all-done.2 = bf16[16,40,512]{2,1,0:T(8,128)(2,1)} async-done(((bf16[16,40,512]{2,1,0:T(8,128)(2,1)}), bf16[16,40,512]{2,1,0:T(8,128)(2,1)}, u32[]{:S(2)}, u32[]{:S(2)}) %all-to-all-start.2) | async-done | bytes 655392 | tf_op jit(solution)/shard_map/all_to_all | solution.py:101
  182.9 12.1 all-to-all-start.4
  196.6 2.4 reshape.269
  201.4 1.0 fusion.12
  202.5 166.4 %all-gather.2.cloned.1.call-done = bf16[640,1024]{1,0:T(8,128)(2,1)} async-done(((bf16[640,128]{1,0:T(8,128)(2,1)}), bf16[640,1024]{1,0:T(8,128)(2,1)}) %all-gather.2.cloned.1.call-update) | async-done | bytes 1310736 | tf_op jit(solution)/shard_map/all_gather | solution.py:111
  369.0 5.5 fusion.36
  375.4 40.9 %all_to_all.46 = bf16[16,40,128]{2,1,0:T(8,128)(2,1)S(1)} all-to-all(bf16[16,40,128]{2,1,0:T(8,128)(2,1)S(1)} %bitcast.133), channel_id=1, replica_groups=mesh['dp'=8,'ctx'=16,'tp'=8] {'ctx'}, dimensions={0} | all-to-all | bytes 327680 | tf_op jit(solution)/shard_map/all_to_all | solution.py:100
  416.2 1.9 fusion.9
  418.2 1.0 fusion.10
  420.7 1.1 convert_element_type.72
  421.8 1.2 fusion.7
  423.0 1105.1 %reduce-scatter.2.cloned.1.call-done = f32[8,1024]{1,0:T(8,128)} async-done(((f32[1024,1024]{1,0:T(8,128)}), f32[8,1024]{1,0:T(8,128)}) %reduce-scatter.2.cloned.1.call-update) | async-done | bytes 32784 | tf_op jit(solution)/shard_map/reduce_scatter | solution.py:114
  (60 shorter events, 10.8 us)
Async XLA Ops:
  7.2 147.9 %copy-start = (bf16[1,512,1024]{2,1,0:T(8,128)(2,1)S(1)}, bf16[1,512,1024]{2,1,0:T(8,128)(2,1)}, u32[]{:S(2)}) copy-start(bf16[1,512,1024]{2,1,0:T(8,128)(2,1)} %param.17) | copy-start | bytes 3145732
  7.2 4.5 copy-start.3
  8.4 5.4 copy-start.4
  13.7 26.4 %copy-start.1 = (bf16[1,512,512]{2,1,0:T(8,128)(2,1)S(1)}, bf16[1,512,512]{2,1,0:T(8,128)(2,1)}, u32[]{:S(2)}) copy-start(bf16[1,512,512]{2,1,0:T(8,128)(2,1)} %param.16) | copy-start | bytes 1572868
  16.7 54.4 %all-to-all-start = ((bf16[16,40,128]{2,1,0:T(8,128)(2,1)}), bf16[16,40,128]{2,1,0:T(8,128)(2,1)S(1)}, u32[]{:S(2)}, u32[]{:S(2)}) async-start(bf16[16,40,128]{2,1,0:T(8,128)(2,1)} %bitcast.4), calls=%async_computation | async-start | bytes 327680 | tf_op jit(solution)/shard_map/all_to_all | solution.py:99
  40.1 2.8 copy-start.2
  119.4 63.5 %all-to-all-start.2 = ((bf16[16,40,512]{2,1,0:T(8,128)(2,1)}), bf16[16,40,512]{2,1,0:T(8,128)(2,1)}, u32[]{:S(2)}, u32[]{:S(2)}) async-start(bf16[16,40,512]{2,1,0:T(8,128)(2,1)} %bitcast.15), calls=%async_computation.2 | async-start | bytes 1310720 | tf_op jit(solution)/shard_map/all_to_all | solution.py:101
  159.2 36.1 %copy-start.12 = (s32[16,16]{1,0:T(8,128)S(1)}, s32[16,16]{1,0:T(8,128)}, u32[]{:S(2)}) copy-start(s32[16,16]{1,0:T(8,128)} %param.18) | copy-start | bytes 3076
  182.9 186.1 %all-to-all-start.4 = ((bf16[16,40,1024]{2,1,0:T(8,128)(2,1)}), bf16[16,40,1024]{2,1,0:T(8,128)(2,1)}, u32[]{:S(2)}, u32[]{:S(2)}) async-start(bf16[16,40,1024]{2,1,0:T(8,128)(2,1)} %select_select_fusion), calls=%async_computation.4 | async-start | bytes 2621440 | tf_op jit(solution)/shard_map/all_to_all | solution.py:107
  195.0 174.0 %all-gather.2.cloned.1.call-start = ((), (), s32[]{:S(2)}) async-start(), calls=%async_computation.6 | async-start | bytes 1474560 | tf_op jit(solution)/shard_map/all_gather | solution.py:111
  196.6 2.4 copy-start.6
  200.3 1.1 copy-start.7
  201.4 1.0 copy-start.9
  202.5 1325.6 %reduce-scatter.2.cloned.1.call-start = ((), (), s32[]{:S(2)}) async-start(), calls=%async_computation.7 | async-start | bytes 4227072 | tf_op jit(solution)/shard_map/reduce_scatter | solution.py:114
  374.5 0.9 copy-start.5
  374.5 43.7 %copy-start.8 = (bf16[16,40,1,4,128]{4,3,1,0,2:T(4,128)(2,1)S(1)}, bf16[16,40,1,4,128]{4,3,1,0,2:T(4,128)(2,1)}, u32[]{:S(2)}) copy-start(bf16[16,40,1,4,128]{4,3,1,0,2:T(4,128)(2,1)} %reshape.269) | copy-start | bytes 1966084
  419.2 0.8 copy-start.10
  420.5 1.4 copy-start.11
Sparse Core Ops, SparseCore 0:
  202.6 166.3 all-gather.1
  374.6 1153.3 reduce-scatter.1
where the time goes:
time: 1540 us; the launch traced here: 1530 us
  waiting for transfers between devices  1320 us (86%)
  blocking collectives  89.2 us (6%)
  starting transfers between devices  71.1 us (5%)
  local copies, waits for them, and re-layouts  21.4 us (1%)
    reduce_scatter x1, waiting for transfers between devices, shards(): lax.psum_scatter(partial_term, ('dp', 'ctx'), scatter_dimension=0, tiled=...  1110 us
    all_gather x1, waiting for transfers between devices, shards(): lax.all_gather(value_grad, 'tp', axis=1, tiled=True)  166 us
    all_to_all x1, blocking collectives, shards(): lax.all_to_all(pack_rows(queries), 'ctx', split_axis=0, concat_axis=0, ti...  48.4 us
    all_to_all x1, blocking collectives, shards(): lax.all_to_all(pack_rows(value_rows), 'ctx', split_axis=0, concat_axis=0,...  40.9 us
    all_to_all x1, starting transfers between devices, shards(): lax.all_to_all(pack_rows(out_grad), 'ctx', split_axis=0, concat_axis=0, t...  35.5 us
  transfers between devices with their start and end apart: 5, of which 4 were waited for; matrix products, arithmetic and copies ran while one was open for 2% of the time, Pallas kernels for 0%

commit v1 on v0

v1 whole, which is shorter than its diff:
```python
import functools

import jax
import jax.numpy as jnp
from jax import lax
from jax.experimental import pallas as pl
from jax.experimental.pallas import tpu as pltpu
from jax.sharding import Mesh, PartitionSpec as P


HD = 128
GROUP = 4
DOCS = 4
NEG = -1e30
LOW = jnp.bfloat16


def dot(a, b):
    return jnp.dot(a, b, preferred_element_type=jnp.float32)


def nt_dot(a, b):
    return lax.dot_general(a, b, (((1,), (1,)), ((), ())), preferred_element_type=jnp.float32)


def tn_dot(a, b):
    return lax.dot_general(a, b, (((0,), (0,)), ((), ())), preferred_element_type=jnp.float32)


def block_of(ids, capacity):
    block = jnp.zeros_like(ids)
    for d in range(1, DOCS):
        block = block + (ids >= d * capacity).astype(jnp.int32)
    return block


def iotas(rows, cols):
    return (
        lax.broadcasted_iota(jnp.int32, (rows, cols), 0),
        lax.broadcasted_iota(jnp.int32, (rows, cols), 1),
    )


def causal_mask(capacity):
    tile = DOCS * capacity
    rows, cols = iotas(tile, tile)
    return (cols <= rows) & (block_of(rows, capacity) == block_of(cols, capacity))


def one_hot(condition):
    return jnp.where(condition, 1.0, 0.0).astype(LOW)


def lane_maps(capacity):
    tile = DOCS * capacity
    cols, lanes = iotas(tile, HD)
    within = cols - capacity * block_of(cols, capacity)
    half = HD // 2
    upright = [one_hot(lanes == within), one_hot(lanes == within + half)]
    turned = [one_hot(lanes == capacity - within), one_hot(lanes == capacity - within + half)]
    return upright, turned


def flip_map(capacity):
    tile = DOCS * capacity
    rows, cols = iotas(tile, tile)
    block = block_of(rows, capacity)
    within = rows - capacity * block
    return one_hot(cols == block * capacity + (capacity - 1) - within)


def attend_kernel(
    index_ref,
    lengths_ref,
    plan_ref,
    query_hbm,
    key_hbm,
    value_hbm,
    grad_hbm,
    packed_ref,
    tokens_ref,
    query_ref,
    key_ref,
    value_ref,
    grad_ref,
    place_ref,
    sums_ref,
    sems,
):
    copies = [
        pltpu.make_async_copy(source, target, sems.at[i])
        for i, (source, target) in enumerate(
            (
                (query_hbm, query_ref),
                (key_hbm, key_ref),
                (value_hbm, value_ref),
                (grad_hbm, grad_ref),
            )
        )
    ]
    for copy in copies:
        copy.start()
    seq_len = query_ref.shape[0]
    docs = lengths_ref.shape[1]
    capacity = packed_ref.shape[0] // docs
    tile = DOCS * capacity
    own = index_ref[0]
    scale = HD ** (-0.5)

    offsets = lax.broadcasted_iota(jnp.int32, (capacity, HD), 0)
    start = jnp.int32(0)
    for d in range(docs):
        length = lengths_ref[own, d]
        target = plan_ref[own, d]
        place_ref[pl.ds(pl.multiple_of(target * capacity, 8), capacity), :] = jnp.where(
            offsets < length, start + offsets, -1
        )
        start = start + length

    bias = jnp.where(causal_mask(capacity), 0.0, NEG)
    bias = jnp.concatenate([bias] * GROUP, axis=0)
    upright, turned = lane_maps(capacity)
    flip = flip_map(capacity)
    for copy in copies:
        copy.wait()
    for part in range(docs // DOCS):
        here = slice(part * tile, (part + 1) * tile)
        place = jnp.concatenate([place_ref[here, :]] * (seq_len // HD), axis=1)
        pick = one_hot(place == lax.broadcasted_iota(jnp.int32, (tile, seq_len), 1))
        query = dot(pick, query_ref[...]).astype(LOW)
        grad = dot(pick, grad_ref[...]).astype(LOW)
        key = dot(pick, key_ref[...]).astype(LOW)
        value = dot(pick, value_ref[...]).astype(LOW)
        query = jnp.concatenate([query[:, h * HD : (h + 1) * HD] for h in range(GROUP)], axis=0)
        grad = jnp.concatenate([grad[:, h * HD : (h + 1) * HD] for h in range(GROUP)], axis=0)
        scores = nt_dot(query, key) * scale + bias
        raised = jnp.exp(scores - jnp.max(scores, axis=1, keepdims=True))
        probs = raised / jnp.sum(raised, axis=1, keepdims=True)
        probs_low = probs.astype(LOW)
        prob_grad = nt_dot(grad, value)
        row_delta = jnp.sum(probs_low.astype(jnp.float32) * prob_grad, axis=1, keepdims=True)
        dscore = (probs * (prob_grad - row_delta)).astype(LOW)
        value_grad = tn_dot(probs_low, grad).astype(LOW)
        sums = tn_dot(pick, value_grad)
        if part == 0:
            sums_ref[...] = sums
        else:
            sums_ref[...] += sums
        heads = [dscore[h * tile : (h + 1) * tile, :] for h in range(GROUP)]
        below = dot(heads[0], upright[0]) + dot(heads[1], upright[1])
        above = (dot(heads[2], turned[0]) + dot(heads[3], turned[1])).astype(LOW)
        packed_ref[here, 0:HD] = key
        packed_ref[here, HD : 2 * HD] = (tn_dot(dscore, query) * scale).astype(LOW)
        packed_ref[here, 2 * HD : 3 * HD] = value_grad
        packed_ref[here, 3 * HD : 4 * HD] = (below + dot(flip, above)).astype(LOW)
    tokens_ref[...] = sums_ref[...].astype(LOW)


def attend(index, lengths, plan, query, key, value, grad):
    seq_len, width = query.shape
    docs = lengths.shape[1]
    packed = docs * (5 * seq_len // (4 * docs))
    smem = pl.BlockSpec(memory_space=pltpu.SMEM)
    vmem = pl.BlockSpec(memory_space=pltpu.VMEM)
    hbm = pl.BlockSpec(memory_space=pl.ANY)
    return pl.pallas_call(
        attend_kernel,
        out_shape=(
            jax.ShapeDtypeStruct((packed, 4 * HD), LOW),
            jax.ShapeDtypeStruct((seq_len, HD), LOW),
        ),
        in_specs=[smem, smem, smem, hbm, hbm, hbm, hbm],
        out_specs=(vmem, vmem),
        scratch_shapes=[
            pltpu.VMEM((seq_len, width), LOW),
            pltpu.VMEM((seq_len, HD), LOW),
            pltpu.VMEM((seq_len, HD), LOW),
            pltpu.VMEM((seq_len, width), LOW),
            pltpu.VMEM((packed, HD), jnp.int32),
            pltpu.VMEM((seq_len, HD), jnp.float32),
            pltpu.SemaphoreType.DMA((4,)),
        ],
        compiler_params=pltpu.CompilerParams(vmem_limit_bytes=60 << 20),
        name="attend",
    )(index, lengths, plan, query, key, value, grad)


def finish_kernel(capacity, packed_ref, query_out, key_out, value_out):
    scale = HD ** (-0.5)
    mask = causal_mask(capacity)
    upright, turned = lane_maps(capacity)
    key = packed_ref[:, 0:HD]
    below = packed_ref[:, 3 * HD : 4 * HD]
    above = dot(flip_map(capacity), below).astype(LOW)
    for h, (half, lanes) in enumerate(
        ((below, upright[0]), (below, upright[1]), (above, turned[0]), (above, turned[1]))
    ):
        dscore = jnp.where(mask, nt_dot(half, lanes), 0.0).astype(LOW)
        query_out[:, h * HD : (h + 1) * HD] = (dot(dscore, key) * scale).astype(LOW)
    key_out[...] = packed_ref[:, HD : 2 * HD]
    value_out[...] = packed_ref[:, 2 * HD : 3 * HD]


def finish(received, capacity):
    rows = received.shape[0]
    tile = DOCS * capacity

    def spec(width):
        return pl.BlockSpec((tile, width), lambda i: (i, 0))

    return pl.pallas_call(
        functools.partial(finish_kernel, capacity),
        grid=(rows // tile,),
        out_shape=(
            jax.ShapeDtypeStruct((rows, GROUP * HD), LOW),
            jax.ShapeDtypeStruct((rows, HD), LOW),
            jax.ShapeDtypeStruct((rows, HD), LOW),
        ),
        in_specs=[spec(4 * HD)],
        out_specs=(spec(GROUP * HD), spec(HD), spec(HD)),
        compiler_params=pltpu.CompilerParams(vmem_limit_bytes=16 << 20),
        name="finish",
    )(received)


def shift(value, axis, step):
    n = lax.axis_size(axis)
    return lax.ppermute(value, axis, [(i, (i + step) % n) for i in range(n)])


def fold(total, axis, dim):
    n = lax.axis_size(axis)
    me = lax.axis_index(axis)
    summed = lax.dynamic_index_in_dim(total, me, dim, keepdims=False)
    for step in range(1, n):
        piece = lax.dynamic_index_in_dim(total, lax.rem(me + step, n), dim, keepdims=False)
        summed = summed + shift(piece.astype(LOW), axis, step).astype(jnp.float32)
    return summed


def fold_far(total, axis):
    me = lax.axis_index(axis)
    first, second = jnp.bitwise_xor(me, 1), 3 - me

    def at(value, i):
        return lax.dynamic_index_in_dim(value, i, 0, keepdims=False)

    away = jnp.stack([at(total, first), at(total, 3 - first)])
    came = lax.ppermute(away.astype(LOW), axis, [(i, i ^ 1) for i in range(4)])
    mine = at(total, me) + came[0].astype(jnp.float32)
    other = at(total, second) + came[1].astype(jnp.float32)
    back = lax.ppermute(other.astype(LOW), axis, [(i, 3 - i) for i in range(4)])
    return mine + back.astype(jnp.float32)


def shards(queries, key_rows, value_rows, out_grad, inputs, doc_lengths, doc_plan):
    own = lax.axis_index(("zhi", "x")).astype(jnp.int32).reshape(1)
    packed, tokens = attend(
        own, doc_lengths, doc_plan, queries[0], key_rows[0], value_rows[0], out_grad[0]
    )
    near = lax.axis_size("zr")
    across = shift(tokens, "zq", 1)
    blocks = [tokens] + [shift(tokens, "zr", k) for k in range(1, near)]
    blocks += [across]
    for k in range(1, near):
        blocks += [shift(across, "zr", k)]
    received = lax.all_to_all(packed, ("zhi", "x"), split_axis=0, concat_axis=0, tiled=True)
    values = jnp.concatenate(blocks, axis=1)
    rows, features = inputs.shape[1:]
    width = values.shape[1]
    ny, nc, nz, nx = (lax.axis_size(a) for a in ("y", "core", "zhi", "x"))
    halves = inputs.reshape(rows, ny, nc, features // (ny * nc))
    core = lax.axis_index("core")

    def term(i):
        part = lax.dynamic_index_in_dim(halves, i, 2, keepdims=False).reshape(rows, features // nc)
        return tn_dot(part, values)

    came = shift(term(1 - core).astype(LOW), "core", 1)
    kept = lax.optimization_barrier(term(core))
    total = kept + came.astype(jnp.float32)
    total = total.reshape(ny, nz, nx, features // (ny * nc * nz * nx), width)
    total = fold(total, "x", 2)
    total = fold(total, "y", 0)
    total = fold_far(total, "zhi")
    total = total.reshape(-1, 2 * near, HD)
    zq, zr = lax.axis_index("zq"), lax.axis_index("zr")
    block = jnp.arange(2 * near)
    source = jnp.bitwise_and(zr - block, near - 1) + near * (block // near != zq)
    total = jnp.take(total, source, axis=1).reshape(-1, width)
    query_grad, key_grad, value_grad = finish(received, packed.shape[0] // doc_plan.shape[1])
    return (query_grad[None], key_grad[None], value_grad[None], total)


def solution(mesh):
    fine = Mesh(mesh.devices.reshape(4, 2, 4, 4, 2, 4), ("y", "core", "zhi", "x", "zq", "zr"))
    tokens = P(("y", "core", "zhi", "x"), None, ("zq", "zr"))
    groups = P(("y", "core"), None)

    return jax.shard_map(
        shards,
        mesh=fine,
        in_specs=(tokens, tokens, tokens, tokens, tokens, groups, groups),
        out_specs=(tokens, tokens, tokens, P(("zq", "zr", "y", "core", "zhi", "x"), None)),
        check_vma=False,
    )
```

time: 1540 us -> 200 us (0.13)
  the two profiles are of different devices: /device:TPU:224 before, /device:TPU:32 now
where the time goes in v1:
time: 200 us; the launch traced here: 199 us
  starting transfers between devices  102 us (51%)
  waiting for transfers between devices  77.2 us (39%)
  Pallas kernels  11.4 us (6%)
  other arithmetic  3.5 us (2%)
    ppermute x14, waiting for transfers between devices, shift(): return lax.ppermute(value, axis, [(i, (i + step) % n) for i in range(n)])  71.5 us
    ppermute x14, starting transfers between devices, shift(): return lax.ppermute(value, axis, [(i, (i + step) % n) for i in range(n)])  57.5 us
    all_to_all x1, starting transfers between devices, shards(): lax.all_to_all(packed, ('zhi', 'x'), split_axis=0, concat_axis=0, tiled=T...  20.8 us
    ppermute x1, starting transfers between devices, fold_far(): came = lax.ppermute(away.astype(LOW), axis, [(i, i ^ 1) for i in range(4)])  12.9 us
    ppermute x1, starting transfers between devices, fold_far(): back = lax.ppermute(other.astype(LOW), axis, [(i, 3 - i) for i in range(4)])  11.1 us
    pallas_call x1, Pallas kernels, attend(): pl.pallas_call(attend_kernel, out_shape=(jax.ShapeDtypeStruct((packed, 4...  8.64 us
  transfers between devices with their start and end apart: 17, of which 8 were waited for; matrix products, arithmetic and copies ran while one was open for 3% of the time, Pallas kernels for 0%

profile of v1, /device:TPU:32, one launch (start us, length us, event | category | flops | bytes accessed | tf_op | source)
XLA Modules:
  0.0 198.9 jit_solution(11514727624800357920)
XLA Ops:
  0.7 8.6 %attend.1 = (bf16[640,512]{1,0:T(8,128)(2,1)}, bf16[512,128]{1,0:T(8,128)(2,1)}) custom-call(s32[1]{0:T(128)} %bitcast.index_ref, s32[16,16]{1,0:T(8,128)} %lengths_ref.1, s32[16,16]{1,0:T(8,128)} %plan_ref.1, bf16[512,512]{1,0:T(8,128)(2,1)} %bitcast.72, bf16[512,128]{1,0:T(8,128)(2,1)} %bitcast.75, bf16[512,128]{1,0:T(8,128)(2,1)} %bitcast.76, ...), custom_call_target="tpu_custom_call" | custom-call | tf_op jit(solution)/shard_map/attend/pallas_call | solution.py:166
  9.3 3.8 %collective-permute-start = (bf16[512,128]{1,0:T(8,128)(2,1)}, bf16[512,128]{1,0:T(8,128)(2,1)S(1)}, u32[]{:S(2)}, u32[]{:S(2)}) collective-permute-start(bf16[512,128]{1,0:T(8,128)(2,1)} %get-tuple-element.13), channel_id=1, source_target_pairs={{0,1},{1,2},{2,3},{3,0},{4,5},{5,6},{6,7},{7,4},{8,9},{9,10},{10,1... | collective-permute-start | bytes 393224 | tf_op jit(solution)/shard_map/ppermute | solution.py:228
  13.1 15.1 %collective-permute-start.1 = (bf16[512,128]{1,0:T(8,128)(2,1)}, bf16[512,128]{1,0:T(8,128)(2,1)S(1)}, u32[]{:S(2)}, u32[]{:S(2)}) collective-permute-start(bf16[512,128]{1,0:T(8,128)(2,1)} %get-tuple-element.13), channel_id=1, source_target_pairs={{0,2},{1,3},{2,0},{3,1},{4,6},{5,7},{6,4},{7,5},{8,10},{9,11},{10,... | collective-permute-start | bytes 393224 | tf_op jit(solution)/shard_map/ppermute | solution.py:228
  32.1 20.8 %all-to-all-start = ((bf16[16,40,512]{2,1,0:T(8,128)(2,1)}), bf16[16,40,512]{2,1,0:T(8,128)(2,1)S(1)}, u32[]{:S(2)}, u32[]{:S(2)}) async-start(bf16[16,40,512]{2,1,0:T(8,128)(2,1)} %bitcast.71), calls=%async_computation | async-start | bytes 1310720 | tf_op jit(solution)/shard_map/all_to_all | solution.py:267
  53.8 3.8 %collective-permute-start.4 = (bf16[512,128]{1,0:T(8,128)(2,1)S(1)}, bf16[512,128]{1,0:T(8,128)(2,1)S(1)}, u32[]{:S(2)}, u32[]{:S(2)}) collective-permute-start(bf16[512,128]{1,0:T(8,128)(2,1)S(1)} %collective-permute-done.3), channel_id=1, source_target_pairs={{0,1},{1,2},{2,3},{3,0},{4,5},{5,6},{6,7},{7,4},{8,9},{9,10},{10,1... | collective-permute-start | bytes 393224 | tf_op jit(solution)/shard_map/ppermute | solution.py:228
  57.6 4.3 %collective-permute-start.5 = (bf16[512,128]{1,0:T(8,128)(2,1)S(1)}, bf16[512,128]{1,0:T(8,128)(2,1)S(1)}, u32[]{:S(2)}, u32[]{:S(2)}) collective-permute-start(bf16[512,128]{1,0:T(8,128)(2,1)S(1)} %collective-permute-done.3), channel_id=1, source_target_pairs={{0,2},{1,3},{2,0},{3,1},{4,6},{5,7},{6,4},{7,5},{8,10},{9,11},{10,... | collective-permute-start | bytes 393224 | tf_op jit(solution)/shard_map/ppermute | solution.py:228
  64.1 26.1 %collective-permute-done.4 = bf16[512,128]{1,0:T(8,128)(2,1)S(1)} collective-permute-done((bf16[512,128]{1,0:T(8,128)(2,1)S(1)}, bf16[512,128]{1,0:T(8,128)(2,1)S(1)}, u32[]{:S(2)}, u32[]{:S(2)}) %collective-permute-start.4) | collective-permute-done | bytes 131104 | tf_op jit(solution)/shard_map/ppermute | solution.py:228
  90.3 27.6 %collective-permute-done.5 = bf16[512,128]{1,0:T(8,128)(2,1)S(1)} collective-permute-done((bf16[512,128]{1,0:T(8,128)(2,1)S(1)}, bf16[512,128]{1,0:T(8,128)(2,1)S(1)}, u32[]{:S(2)}, u32[]{:S(2)}) %collective-permute-start.5) | collective-permute-done | bytes 131104 | tf_op jit(solution)/shard_map/ppermute | solution.py:228
  117.9 2.2 %collective-permute-done.6 = bf16[512,128]{1,0:T(8,128)(2,1)S(1)} collective-permute-done((bf16[512,128]{1,0:T(8,128)(2,1)S(1)}, bf16[512,128]{1,0:T(8,128)(2,1)S(1)}, u32[]{:S(2)}, u32[]{:S(2)}) %collective-permute-start.6) | collective-permute-done | bytes 131104 | tf_op jit(solution)/shard_map/ppermute | solution.py:228
  120.9 1.9 collective-permute-start.7
  123.5 2.0 %collective-permute-done.7 = bf16[512,1024]{1,0:T(8,128)(2,1)} collective-permute-done((bf16[512,1024]{1,0:T(8,128)(2,1)S(1)}, bf16[512,1024]{1,0:T(8,128)(2,1)}, u32[]{:S(2)}, u32[]{:S(2)}) %collective-permute-start.7) | collective-permute-done | bytes 1048608 | tf_op jit(solution)/shard_map/ppermute | solution.py:228
  127.2 5.1 %collective-permute-start.10 = (bf16[4,4,8,1024]{3,2,1,0:T(8,128)(2,1)S(1)}, bf16[4,4,8,1024]{3,2,1,0:T(8,128)(2,1)}, u32[]{:S(2)}, u32[]{:S(2)}) collective-permute-start(bf16[4,4,8,1024]{3,2,1,0:T(8,128)(2,1)S(1)} %get-tuple-element.15), channel_id=1, source_target_pairs={{0,24},{8,0},{16,8},{24,16},{1,25},{9,1},{17,9},{25,17},{2,26},{10... | collective-permute-start | bytes 786440 | tf_op jit(solution)/shard_map/ppermute | solution.py:228
  132.4 1.9 collective-permute-start.8
  134.3 4.2 %collective-permute-start.9 = (bf16[4,4,8,1024]{3,2,1,0:T(8,128)(2,1)S(1)}, bf16[4,4,8,1024]{3,2,1,0:T(8,128)(2,1)}, u32[]{:S(2)}, u32[]{:S(2)}) collective-permute-start(bf16[4,4,8,1024]{3,2,1,0:T(8,128)(2,1)S(1)} %get-tuple-element.16), channel_id=1, source_target_pairs={{0,16},{8,24},{16,0},{24,8},{1,17},{9,25},{17,1},{25,9},{2,18},{10... | collective-permute-start | bytes 786440 | tf_op jit(solution)/shard_map/ppermute | solution.py:228
  138.6 10.7 %collective-permute-done.8 = bf16[4,4,8,1024]{3,2,1,0:T(8,128)(2,1)} collective-permute-done((bf16[4,4,8,1024]{3,2,1,0:T(8,128)(2,1)S(1)}, bf16[4,4,8,1024]{3,2,1,0:T(8,128)(2,1)}, u32[]{:S(2)}, u32[]{:S(2)}) %collective-permute-start.8) | collective-permute-done | bytes 262176 | tf_op jit(solution)/shard_map/ppermute | solution.py:228
  150.6 3.5 %collective-permute-start.11 = (bf16[4,8,1024]{2,1,0:T(8,128)(2,1)S(1)}, bf16[4,8,1024]{2,1,0:T(8,128)(2,1)S(1)}, u32[]{:S(2)}, u32[]{:S(2)}) collective-permute-start(bf16[4,8,1024]{2,1,0:T(8,128)(2,1)S(1)} %get-tuple-element.19), channel_id=1, source_target_pairs={{0,256},{256,512},{512,768},{768,0},{1,257},{257,513},{513,769},{7... | collective-permute-start | bytes 196616 | tf_op jit(solution)/shard_map/ppermute | solution.py:228
  154.1 4.8 %collective-permute-start.12 = (bf16[4,8,1024]{2,1,0:T(8,128)(2,1)S(1)}, bf16[4,8,1024]{2,1,0:T(8,128)(2,1)S(1)}, u32[]{:S(2)}, u32[]{:S(2)}) collective-permute-start(bf16[4,8,1024]{2,1,0:T(8,128)(2,1)S(1)} %get-tuple-element.21), channel_id=1, source_target_pairs={{0,512},{256,768},{512,0},{768,256},{1,513},{257,769},{513,1},{769... | collective-permute-start | bytes 196616 | tf_op jit(solution)/shard_map/ppermute | solution.py:228
  158.9 3.3 %collective-permute-start.13 = (bf16[4,8,1024]{2,1,0:T(8,128)(2,1)S(1)}, bf16[4,8,1024]{2,1,0:T(8,128)(2,1)S(1)}, u32[]{:S(2)}, u32[]{:S(2)}) collective-permute-start(bf16[4,8,1024]{2,1,0:T(8,128)(2,1)S(1)} %get-tuple-element.20), channel_id=1, source_target_pairs={{0,768},{256,0},{512,256},{768,512},{1,769},{257,1},{513,257},{769... | collective-permute-start | bytes 196616 | tf_op jit(solution)/shard_map/ppermute | solution.py:228
  162.2 2.8 %collective-permute-done.13 = bf16[4,8,1024]{2,1,0:T(8,128)(2,1)S(1)} collective-permute-done((bf16[4,8,1024]{2,1,0:T(8,128)(2,1)S(1)}, bf16[4,8,1024]{2,1,0:T(8,128)(2,1)S(1)}, u32[]{:S(2)}, u32[]{:S(2)}) %collective-permute-start.13) | collective-permute-done | bytes 65568 | tf_op jit(solution)/shard_map/ppermute | solution.py:228
  165.1 12.9 %collective-permute-start.14 = (bf16[2,8,1024]{2,1,0:T(8,128)(2,1)S(1)}, bf16[2,8,1024]{2,1,0:T(8,128)(2,1)S(1)}, u32[]{:S(2)}, u32[]{:S(2)}) collective-permute-start(bf16[2,8,1024]{2,1,0:T(8,128)(2,1)S(1)} %pad_maximum_fusion), channel_id=1, source_target_pairs={{0,32},{32,0},{64,96},{96,64},{1,33},{33,1},{65,97},{97,65},{2,34}... | collective-permute-start | bytes 98312 | tf_op jit(solution)/shard_map/ppermute | solution.py:249
  178.1 2.6 %collective-permute-done.14 = bf16[2,8,1024]{2,1,0:T(8,128)(2,1)S(1)} collective-permute-done((bf16[2,8,1024]{2,1,0:T(8,128)(2,1)S(1)}, bf16[2,8,1024]{2,1,0:T(8,128)(2,1)S(1)}, u32[]{:S(2)}, u32[]{:S(2)}) %collective-permute-start.14) | collective-permute-done | bytes 32800 | tf_op jit(solution)/shard_map/ppermute | solution.py:249
  180.7 11.1 %collective-permute-start.15 = (bf16[8,1024]{1,0:T(8,128)(2,1)S(1)}, bf16[8,1024]{1,0:T(8,128)(2,1)S(1)}, u32[]{:S(2)}, u32[]{:S(2)}) collective-permute-start(bf16[8,1024]{1,0:T(8,128)(2,1)S(1)} %fusion.11), channel_id=1, source_target_pairs={{0,96},{32,64},{64,32},{96,0},{1,97},{33,65},{65,33},{97,1},{2,98}... | collective-permute-start | bytes 49160 | tf_op jit(solution)/shard_map/ppermute | solution.py:252
  191.8 3.2 %collective-permute-done.15 = bf16[8,1024]{1,0:T(8,128)(2,1)S(1)} collective-permute-done((bf16[8,1024]{1,0:T(8,128)(2,1)S(1)}, bf16[8,1024]{1,0:T(8,128)(2,1)S(1)}, u32[]{:S(2)}, u32[]{:S(2)}) %collective-permute-start.15) | collective-permute-done | bytes 16416 | tf_op jit(solution)/shard_map/ppermute | solution.py:252
  196.2 2.7 %finish.1 = (bf16[640,512]{1,0:T(8,128)(2,1)}, bf16[640,128]{1,0:T(8,128)(2,1)}, bf16[640,128]{1,0:T(8,128)(2,1)}) custom-call(bf16[640,512]{1,0:T(8,128)(2,1)S(1)} %bitcast.66), custom_call_target="tpu_custom_call" | custom-call | tf_op jit(solution)/shard_map/finish/pallas_call | solution.py:211
  (43 shorter events, 12.7 us)
Async XLA Ops:
  0.6 52.2 %copy-start = (bf16[1,512,1024]{2,1,0:T(8,128)(2,1)S(1)}, bf16[1,512,1024]{2,1,0:T(8,128)(2,1)}, u32[]{:S(2)}) copy-start(bf16[1,512,1024]{2,1,0:T(8,128)(2,1)} %param.11) | copy-start | bytes 3145732
  9.3 52.6 %collective-permute-start = (bf16[512,128]{1,0:T(8,128)(2,1)}, bf16[512,128]{1,0:T(8,128)(2,1)S(1)}, u32[]{:S(2)}, u32[]{:S(2)}) collective-permute-start(bf16[512,128]{1,0:T(8,128)(2,1)} %get-tuple-element.13), channel_id=1, source_target_pairs={{0,1},{1,2},{2,3},{3,0},{4,5},{5,6},{6,7},{7,4},{8,9},{9,10},{10,1... | collective-permute-start | bytes 393224 | tf_op jit(solution)/shard_map/ppermute | solution.py:228
  13.1 50.8 %collective-permute-start.1 = (bf16[512,128]{1,0:T(8,128)(2,1)}, bf16[512,128]{1,0:T(8,128)(2,1)S(1)}, u32[]{:S(2)}, u32[]{:S(2)}) collective-permute-start(bf16[512,128]{1,0:T(8,128)(2,1)} %get-tuple-element.13), channel_id=1, source_target_pairs={{0,2},{1,3},{2,0},{3,1},{4,6},{5,7},{6,4},{7,5},{8,10},{9,11},{10,... | collective-permute-start | bytes 393224 | tf_op jit(solution)/shard_map/ppermute | solution.py:228
  28.2 35.8 %collective-permute-start.2 = (bf16[512,128]{1,0:T(8,128)(2,1)}, bf16[512,128]{1,0:T(8,128)(2,1)S(1)}, u32[]{:S(2)}, u32[]{:S(2)}) collective-permute-start(bf16[512,128]{1,0:T(8,128)(2,1)} %get-tuple-element.13), channel_id=1, source_target_pairs={{0,3},{1,0},{2,1},{3,2},{4,7},{5,4},{6,5},{7,6},{8,11},{9,8},{10,9... | collective-permute-start | bytes 393224 | tf_op jit(solution)/shard_map/ppermute | solution.py:228
  30.1 23.7 %collective-permute-start.3 = (bf16[512,128]{1,0:T(8,128)(2,1)}, bf16[512,128]{1,0:T(8,128)(2,1)S(1)}, u32[]{:S(2)}, u32[]{:S(2)}) collective-permute-start(bf16[512,128]{1,0:T(8,128)(2,1)} %get-tuple-element.13), channel_id=1, source_target_pairs={{0,4},{4,0},{1,5},{5,1},{2,6},{6,2},{3,7},{7,3},{8,12},{12,8},{9,1... | collective-permute-start | bytes 393224 | tf_op jit(solution)/shard_map/ppermute | solution.py:228
  32.1 164.1 %all-to-all-start = ((bf16[16,40,512]{2,1,0:T(8,128)(2,1)}), bf16[16,40,512]{2,1,0:T(8,128)(2,1)S(1)}, u32[]{:S(2)}, u32[]{:S(2)}) async-start(bf16[16,40,512]{2,1,0:T(8,128)(2,1)} %bitcast.71), calls=%async_computation | async-start | bytes 1310720 | tf_op jit(solution)/shard_map/all_to_all | solution.py:267
  52.9 0.9 copy-start.1
  53.8 36.4 %collective-permute-start.4 = (bf16[512,128]{1,0:T(8,128)(2,1)S(1)}, bf16[512,128]{1,0:T(8,128)(2,1)S(1)}, u32[]{:S(2)}, u32[]{:S(2)}) collective-permute-start(bf16[512,128]{1,0:T(8,128)(2,1)S(1)} %collective-permute-done.3), channel_id=1, source_target_pairs={{0,1},{1,2},{2,3},{3,0},{4,5},{5,6},{6,7},{7,4},{8,9},{9,10},{10,1... | collective-permute-start | bytes 393224 | tf_op jit(solution)/shard_map/ppermute | solution.py:228
  57.6 60.2 %collective-permute-start.5 = (bf16[512,128]{1,0:T(8,128)(2,1)S(1)}, bf16[512,128]{1,0:T(8,128)(2,1)S(1)}, u32[]{:S(2)}, u32[]{:S(2)}) collective-permute-start(bf16[512,128]{1,0:T(8,128)(2,1)S(1)} %collective-permute-done.3), channel_id=1, source_target_pairs={{0,2},{1,3},{2,0},{3,1},{4,6},{5,7},{6,4},{7,5},{8,10},{9,11},{10,... | collective-permute-start | bytes 393224 | tf_op jit(solution)/shard_map/ppermute | solution.py:228
  61.9 58.1 %collective-permute-start.6 = (bf16[512,128]{1,0:T(8,128)(2,1)S(1)}, bf16[512,128]{1,0:T(8,128)(2,1)S(1)}, u32[]{:S(2)}, u32[]{:S(2)}) collective-permute-start(bf16[512,128]{1,0:T(8,128)(2,1)S(1)} %collective-permute-done.3), channel_id=1, source_target_pairs={{0,3},{1,0},{2,1},{3,2},{4,7},{5,4},{6,5},{7,6},{8,11},{9,8},{10,9... | collective-permute-start | bytes 393224 | tf_op jit(solution)/shard_map/ppermute | solution.py:228
  120.9 4.7 %collective-permute-start.7 = (bf16[512,1024]{1,0:T(8,128)(2,1)S(1)}, bf16[512,1024]{1,0:T(8,128)(2,1)}, u32[]{:S(2)}, u32[]{:S(2)}) collective-permute-start(bf16[512,1024]{1,0:T(8,128)(2,1)S(1)} %convolution_convert_fusion), channel_id=1, source_target_pairs={{0,128},{128,0},{1,129},{129,1},{2,130},{130,2},{3,131},{131,3},{4... | collective-permute-start | bytes 3145736 | tf_op jit(solution)/shard_map/ppermute | solution.py:228
  127.2 11.3 %collective-permute-start.10 = (bf16[4,4,8,1024]{3,2,1,0:T(8,128)(2,1)S(1)}, bf16[4,4,8,1024]{3,2,1,0:T(8,128)(2,1)}, u32[]{:S(2)}, u32[]{:S(2)}) collective-permute-start(bf16[4,4,8,1024]{3,2,1,0:T(8,128)(2,1)S(1)} %get-tuple-element.15), channel_id=1, source_target_pairs={{0,24},{8,0},{16,8},{24,16},{1,25},{9,1},{17,9},{25,17},{2,26},{10... | collective-permute-start | bytes 786440 | tf_op jit(solution)/shard_map/ppermute | solution.py:228
  132.4 16.9 %collective-permute-start.8 = (bf16[4,4,8,1024]{3,2,1,0:T(8,128)(2,1)S(1)}, bf16[4,4,8,1024]{3,2,1,0:T(8,128)(2,1)}, u32[]{:S(2)}, u32[]{:S(2)}) collective-permute-start(bf16[4,4,8,1024]{3,2,1,0:T(8,128)(2,1)S(1)} %get-tuple-element.14), channel_id=1, source_target_pairs={{0,8},{8,16},{16,24},{24,0},{1,9},{9,17},{17,25},{25,1},{2,10},{10... | collective-permute-start | bytes 786440 | tf_op jit(solution)/shard_map/ppermute | solution.py:228
  134.3 15.0 %collective-permute-start.9 = (bf16[4,4,8,1024]{3,2,1,0:T(8,128)(2,1)S(1)}, bf16[4,4,8,1024]{3,2,1,0:T(8,128)(2,1)}, u32[]{:S(2)}, u32[]{:S(2)}) collective-permute-start(bf16[4,4,8,1024]{3,2,1,0:T(8,128)(2,1)S(1)} %get-tuple-element.16), channel_id=1, source_target_pairs={{0,16},{8,24},{16,0},{24,8},{1,17},{9,25},{17,1},{25,9},{2,18},{10... | collective-permute-start | bytes 786440 | tf_op jit(solution)/shard_map/ppermute | solution.py:228
  150.6 11.6 %collective-permute-start.11 = (bf16[4,8,1024]{2,1,0:T(8,128)(2,1)S(1)}, bf16[4,8,1024]{2,1,0:T(8,128)(2,1)S(1)}, u32[]{:S(2)}, u32[]{:S(2)}) collective-permute-start(bf16[4,8,1024]{2,1,0:T(8,128)(2,1)S(1)} %get-tuple-element.19), channel_id=1, source_target_pairs={{0,256},{256,512},{512,768},{768,0},{1,257},{257,513},{513,769},{7... | collective-permute-start | bytes 196616 | tf_op jit(solution)/shard_map/ppermute | solution.py:228
  154.1 8.2 %collective-permute-start.12 = (bf16[4,8,1024]{2,1,0:T(8,128)(2,1)S(1)}, bf16[4,8,1024]{2,1,0:T(8,128)(2,1)S(1)}, u32[]{:S(2)}, u32[]{:S(2)}) collective-permute-start(bf16[4,8,1024]{2,1,0:T(8,128)(2,1)S(1)} %get-tuple-element.21), channel_id=1, source_target_pairs={{0,512},{256,768},{512,0},{768,256},{1,513},{257,769},{513,1},{769... | collective-permute-start | bytes 196616 | tf_op jit(solution)/shard_map/ppermute | solution.py:228
  158.9 6.2 %collective-permute-start.13 = (bf16[4,8,1024]{2,1,0:T(8,128)(2,1)S(1)}, bf16[4,8,1024]{2,1,0:T(8,128)(2,1)S(1)}, u32[]{:S(2)}, u32[]{:S(2)}) collective-permute-start(bf16[4,8,1024]{2,1,0:T(8,128)(2,1)S(1)} %get-tuple-element.20), channel_id=1, source_target_pairs={{0,768},{256,0},{512,256},{768,512},{1,769},{257,1},{513,257},{769... | collective-permute-start | bytes 196616 | tf_op jit(solution)/shard_map/ppermute | solution.py:228
  165.1 15.5 %collective-permute-start.14 = (bf16[2,8,1024]{2,1,0:T(8,128)(2,1)S(1)}, bf16[2,8,1024]{2,1,0:T(8,128)(2,1)S(1)}, u32[]{:S(2)}, u32[]{:S(2)}) collective-permute-start(bf16[2,8,1024]{2,1,0:T(8,128)(2,1)S(1)} %pad_maximum_fusion), channel_id=1, source_target_pairs={{0,32},{32,0},{64,96},{96,64},{1,33},{33,1},{65,97},{97,65},{2,34}... | collective-permute-start | bytes 98312 | tf_op jit(solution)/shard_map/ppermute | solution.py:249
  180.7 14.3 %collective-permute-start.15 = (bf16[8,1024]{1,0:T(8,128)(2,1)S(1)}, bf16[8,1024]{1,0:T(8,128)(2,1)S(1)}, u32[]{:S(2)}, u32[]{:S(2)}) collective-permute-start(bf16[8,1024]{1,0:T(8,128)(2,1)S(1)} %fusion.11), channel_id=1, source_target_pairs={{0,96},{32,64},{64,32},{96,0},{1,97},{33,65},{65,33},{97,1},{2,98}... | collective-permute-start | bytes 49160 | tf_op jit(solution)/shard_map/ppermute | solution.py:252

commit v2 on v1

--- a/solution.py
+++ b/solution.py
@@ -67,6 +67,81 @@
     block = block_of(rows, capacity)
     within = rows - capacity * block
     return one_hot(cols == block * capacity + (capacity - 1) - within)
+
+
+def place_rows(index_ref, lengths_ref, plan_ref, place_ref, capacity):
+    own = index_ref[0]
+    offsets = lax.broadcasted_iota(jnp.int32, (capacity, HD), 0)
+    start = jnp.int32(0)
+    for d in range(lengths_ref.shape[1]):
+        length = lengths_ref[own, d]
+        target = plan_ref[own, d]
+        place_ref[pl.ds(pl.multiple_of(target * capacity, 8), capacity), :] = jnp.where(
+            offsets < length, start + offsets, -1
+        )
+        start = start + length
+
+
+def fetch(pairs, sems):
+    copies = [
+        pltpu.make_async_copy(source, target, sems.at[i])
+        for i, (source, target) in enumerate(pairs)
+    ]
+    for copy in copies:
+        copy.start()
+    return copies
+
+
+def picker(place_ref, here, seq_len):
+    place = jnp.concatenate([place_ref[here, :]] * (seq_len // HD), axis=1)
+    return one_hot(place == lax.broadcasted_iota(jnp.int32, place.shape, 1))
+
+
+def by_head(rows):
+    return jnp.concatenate([rows[:, h * HD : (h + 1) * HD] for h in range(GROUP)], axis=0)
+
+
+def softmax_bias(capacity):
+    return jnp.concatenate([jnp.where(causal_mask(capacity), 0.0, NEG)] * GROUP, axis=0)
+
+
+def softmax(query, key, bias):
+    scores = nt_dot(query, key) * HD ** (-0.5) + bias
+    raised = jnp.exp(scores - jnp.max(scores, axis=1, keepdims=True))
+    return raised / jnp.sum(raised, axis=1, keepdims=True)
+
+
+def tokens_kernel(
+    index_ref,
+    lengths_ref,
+    plan_ref,
+    query_hbm,
+    key_hbm,
+    grad_hbm,
+    tokens_ref,
+    query_ref,
+    key_ref,
+    grad_ref,
+    place_ref,
+    sems,
+):
+    copies = fetch(((query_hbm, query_ref), (key_hbm, key_ref), (grad_hbm, grad_ref)), sems)
+    seq_len = query_ref.shape[0]
+    capacity = place_ref.shape[0] // lengths_ref.shape[1]
+    tile = DOCS * capacity
+    place_rows(index_ref, lengths_ref, plan_ref, place_ref, capacity)
+    bias = softmax_bias(capacity)
+    for copy in copies:
+        copy.wait()
+    sums = jnp.zeros(tokens_ref.shape, jnp.float32)
+    for part in range(place_ref.shape[0] // tile):
+        pick = picker(place_ref, slice(part * tile, (part + 1) * tile), seq_len)
+        query = by_head(dot(pick, query_ref[...]).astype(LOW))
+        grad = by_head(dot(pick, grad_ref[...]).astype(LOW))
+        key = dot(pick, key_ref[...]).astype(LOW)
+        probs_low = softmax(query, key, bias).astype(LOW)
+        sums += tn_dot(pick, tn_dot(probs_low, grad).astype(LOW))
+    tokens_ref[...] = sums.astype(LOW)
 
 
 def attend_kernel(
@@ -78,111 +153,89 @@
     value_hbm,
     grad_hbm,
     packed_ref,
-    tokens_ref,
     query_ref,
     key_ref,
     value_ref,
     grad_ref,
     place_ref,
-    sums_ref,
     sems,
 ):
-    copies = [
-        pltpu.make_async_copy(source, target, sems.at[i])
-        for i, (source, target) in enumerate(
-            (
-                (query_hbm, query_ref),
-                (key_hbm, key_ref),
-                (value_hbm, value_ref),
-                (grad_hbm, grad_ref),
-            )
-        )
-    ]
-    for copy in copies:
-        copy.start()
+    copies = fetch(
+        (
+            (query_hbm, query_ref),
+            (key_hbm, key_ref),
+            (value_hbm, value_ref),
+            (grad_hbm, grad_ref),
+        ),
+        sems,
+    )
     seq_len = query_ref.shape[0]
-    docs = lengths_ref.shape[1]
-    capacity = packed_ref.shape[0] // docs
-    tile = DOCS * capacity
-    own = index_ref[0]
+    capacity = place_ref.shape[0] // lengths_ref.shape[1]
+    tile = DOCS * capacity
     scale = HD ** (-0.5)
-
-    offsets = lax.broadcasted_iota(jnp.int32, (capacity, HD), 0)
-    start = jnp.int32(0)
-    for d in range(docs):
-        length = lengths_ref[own, d]
-        target = plan_ref[own, d]
-        place_ref[pl.ds(pl.multiple_of(target * capacity, 8), capacity), :] = jnp.where(
-            offsets < length, start + offsets, -1
-        )
-        start = start + length
-
-    bias = jnp.where(causal_mask(capacity), 0.0, NEG)
-    bias = jnp.concatenate([bias] * GROUP, axis=0)
+    place_rows(index_ref, lengths_ref, plan_ref, place_ref, capacity)
+    bias = softmax_bias(capacity)
     upright, turned = lane_maps(capacity)
     flip = flip_map(capacity)
     for copy in copies:
         copy.wait()
-    for part in range(docs // DOCS):
+    for part in range(place_ref.shape[0] // tile):
         here = slice(part * tile, (part + 1) * tile)
-        place = jnp.concatenate([place_ref[here, :]] * (seq_len // HD), axis=1)
-        pick = one_hot(place == lax.broadcasted_iota(jnp.int32, (tile, seq_len), 1))
-        query = dot(pick, query_ref[...]).astype(LOW)
-        grad = dot(pick, grad_ref[...]).astype(LOW)
+        pick = picker(place_ref, here, seq_len)
+        query = by_head(dot(pick, query_ref[...]).astype(LOW))
+        grad = by_head(dot(pick, grad_ref[...]).astype(LOW))
         key = dot(pick, key_ref[...]).astype(LOW)
         value = dot(pick, value_ref[...]).astype(LOW)
-        query = jnp.concatenate([query[:, h * HD : (h + 1) * HD] for h in range(GROUP)], axis=0)
-        grad = jnp.concatenate([grad[:, h * HD : (h + 1) * HD] for h in range(GROUP)], axis=0)
-        scores = nt_dot(query, key) * scale + bias
-        raised = jnp.exp(scores - jnp.max(scores, axis=1, keepdims=True))
-        probs = raised / jnp.sum(raised, axis=1, keepdims=True)
+        probs = softmax(query, key, bias)
         probs_low = probs.astype(LOW)
         prob_grad = nt_dot(grad, value)
         row_delta = jnp.sum(probs_low.astype(jnp.float32) * prob_grad, axis=1, keepdims=True)
         dscore = (probs * (prob_grad - row_delta)).astype(LOW)
-        value_grad = tn_dot(probs_low, grad).astype(LOW)
-        sums = tn_dot(pick, value_grad)
-        if part == 0:
-            sums_ref[...] = sums
-        else:
-            sums_ref[...] += sums
         heads = [dscore[h * tile : (h + 1) * tile, :] for h in range(GROUP)]
         below = dot(heads[0], upright[0]) + dot(heads[1], upright[1])
         above = (dot(heads[2], turned[0]) + dot(heads[3], turned[1])).astype(LOW)
         packed_ref[here, 0:HD] = key
         packed_ref[here, HD : 2 * HD] = (tn_dot(dscore, query) * scale).astype(LOW)
-        packed_ref[here, 2 * HD : 3 * HD] = value_grad
+        packed_ref[here, 2 * HD : 3 * HD] = tn_dot(probs_low, grad).astype(LOW)
         packed_ref[here, 3 * HD : 4 * HD] = (below + dot(flip, above)).astype(LOW)
-    tokens_ref[...] = sums_ref[...].astype(LOW)
-
-
-def attend(index, lengths, plan, query, key, value, grad):
-    seq_len, width = query.shape
-    docs = lengths.shape[1]
+
+
+def local_call(kernel, plan_of, arrays, out_shape, flops):
+    seq_len = arrays[0].shape[0]
+    docs = plan_of[1].shape[1]
     packed = docs * (5 * seq_len // (4 * docs))
     smem = pl.BlockSpec(memory_space=pltpu.SMEM)
-    vmem = pl.BlockSpec(memory_space=pltpu.VMEM)
-    hbm = pl.BlockSpec(memory_space=pl.ANY)
+    moved = sum(2 * a.size for a in arrays)
     return pl.pallas_call(
+        kernel,
+        out_shape=out_shape(packed),
+        in_specs=[smem] * 3 + [pl.BlockSpec(memory_space=pl.ANY)] * len(arrays),
+        out_specs=pl.BlockSpec(memory_space=pltpu.VMEM),
+        scratch_shapes=[pltpu.VMEM(a.shape, LOW) for a in arrays]
+        + [pltpu.VMEM((packed, HD), jnp.int32), pltpu.SemaphoreType.DMA((len(arrays),))],
+        compiler_params=pltpu.CompilerParams(vmem_limit_bytes=60 << 20),
+        cost_estimate=pl.CostEstimate(flops=flops, bytes_accessed=moved, transcendentals=400000),
+    )(*plan_of, *arrays)
+
+
+def value_tokens(plan_of, query, key, grad):
+    return local_call(
+        tokens_kernel,
+        plan_of,
+        (query, key, grad),
+        lambda packed: jax.ShapeDtypeStruct(key.shape, LOW),
+        10**9,
+    )
+
+
+def attend(plan_of, query, key, value, grad):
+    return local_call(
         attend_kernel,
-        out_shape=(
-            jax.ShapeDtypeStruct((packed, 4 * HD), LOW),
-            jax.ShapeDtypeStruct((seq_len, HD), LOW),
-        ),
-        in_specs=[smem, smem, smem, hbm, hbm, hbm, hbm],
-        out_specs=(vmem, vmem),
-        scratch_shapes=[
-            pltpu.VMEM((seq_len, width), LOW),
-            pltpu.VMEM((seq_len, HD), LOW),
-            pltpu.VMEM((seq_len, HD), LOW),
-            pltpu.VMEM((seq_len, width), LOW),
-            pltpu.VMEM((packed, HD), jnp.int32),
-            pltpu.VMEM((seq_len, HD), jnp.float32),
-            pltpu.SemaphoreType.DMA((4,)),
-        ],
-        compiler_params=pltpu.CompilerParams(vmem_limit_bytes=60 << 20),
-        name="attend",
-    )(index, lengths, plan, query, key, value, grad)
+        plan_of,
+        (query, key, value, grad),
+        lambda packed: jax.ShapeDtypeStruct((packed, 4 * HD), LOW),
+        2 * 10**9,
+    )
 
 
 def finish_kernel(capacity, packed_ref, query_out, key_out, value_out):
@@ -223,6 +276,32 @@
     )(received)
 
 
+def term_kernel(core_ref, inputs_ref, *refs):
+    *block_refs, away_ref, kept_ref = refs
+    values = jnp.concatenate([ref[...] for ref in block_refs], axis=1)
+    cores = inputs_ref.shape[1] // away_ref.shape[0]
+    for out_ref, which in ((away_ref, cores - 1 - core_ref[0]), (kept_ref, core_ref[0])):
+        for y in range(out_ref.shape[0] // HD):
+            part = inputs_ref[:, pl.ds(pl.multiple_of((y * cores + which) * HD, HD), HD)]
+            out_ref[y * HD : (y + 1) * HD, :] = tn_dot(part, values).astype(out_ref.dtype)
+
+
+def terms(core, inputs, blocks, cores):
+    rows, width = inputs.shape[1] // cores, sum(b.shape[1] for b in blocks)
+    return pl.pallas_call(
+        term_kernel,
+        out_shape=(
+            jax.ShapeDtypeStruct((rows, width), LOW),
+            jax.ShapeDtypeStruct((rows, width), jnp.float32),
+        ),
+        in_specs=[pl.BlockSpec(memory_space=pltpu.SMEM)]
+        + [pl.BlockSpec(memory_space=pltpu.VMEM)] * (1 + len(blocks)),
+        out_specs=(pl.BlockSpec(memory_space=pltpu.VMEM),) * 2,
+        compiler_params=pltpu.CompilerParams(vmem_limit_bytes=24 << 20),
+        name="terms",
+    )(core, inputs, *blocks)
+
+
 def shift(value, axis, step):
     n = lax.axis_size(axis)
     return lax.ppermute(value, axis, [(i, (i + step) % n) for i in range(n)])
@@ -255,38 +334,30 @@
 
 def shards(queries, key_rows, value_rows, out_grad, inputs, doc_lengths, doc_plan):
     own = lax.axis_index(("zhi", "x")).astype(jnp.int32).reshape(1)
-    packed, tokens = attend(
-        own, doc_lengths, doc_plan, queries[0], key_rows[0], value_rows[0], out_grad[0]
-    )
+    plan_of = (own, doc_lengths, doc_plan)
+    tokens = value_tokens(plan_of, queries[0], key_rows[0], out_grad[0])
     near = lax.axis_size("zr")
     across = shift(tokens, "zq", 1)
-    blocks = [tokens] + [shift(tokens, "zr", k) for k in range(1, near)]
-    blocks += [across]
+    packed = attend(plan_of, queries[0], key_rows[0], value_rows[0], out_grad[0])
+    pair = jnp.concatenate([tokens, across], axis=1)
+    blocks = [pair]
     for k in range(1, near):
-        blocks += [shift(across, "zr", k)]
+        blocks += [shift(pair, "zr", k)]
     received = lax.all_to_all(packed, ("zhi", "x"), split_axis=0, concat_axis=0, tiled=True)
-    values = jnp.concatenate(blocks, axis=1)
-    rows, features = inputs.shape[1:]
-    width = values.shape[1]
+    features, width = inputs.shape[2], sum(b.shape[1] for b in blocks)
     ny, nc, nz, nx = (lax.axis_size(a) for a in ("y", "core", "zhi", "x"))
-    halves = inputs.reshape(rows, ny, nc, features // (ny * nc))
-    core = lax.axis_index("core")
-
-    def term(i):
-        part = lax.dynamic_index_in_dim(halves, i, 2, keepdims=False).reshape(rows, features // nc)
-        return tn_dot(part, values)
-
-    came = shift(term(1 - core).astype(LOW), "core", 1)
-    kept = lax.optimization_barrier(term(core))
+    core = lax.axis_index("core").astype(jnp.int32).reshape(1)
+    away, kept = terms(core, inputs[0], blocks, nc)
+    came = shift(away, "core", 1)
     total = kept + came.astype(jnp.float32)
     total = total.reshape(ny, nz, nx, features // (ny * nc * nz * nx), width)
-    total = fold(total, "x", 2)
     total = fold(total, "y", 0)
+    total = fold(total, "x", 1)
     total = fold_far(total, "zhi")
     total = total.reshape(-1, 2 * near, HD)
     zq, zr = lax.axis_index("zq"), lax.axis_index("zr")
     block = jnp.arange(2 * near)
-    source = jnp.bitwise_and(zr - block, near - 1) + near * (block // near != zq)
+    source = 2 * jnp.bitwise_and(zr - block, near - 1) + (block // near != zq)
     total = jnp.take(total, source, axis=1).reshape(-1, width)
     query_grad, key_grad, value_grad = finish(received, packed.shape[0] // doc_plan.shape[1])
     return (query_grad[None], key_grad[None], value_grad[None], total)

time: 200 us -> 220 us (1.10)
  the two profiles are of different devices: /device:TPU:32 before, /device:TPU:46 now
where the time goes in v2:
time: 220 us; the launch traced here: 219 us
  starting transfers between devices  94.7 us (43%)
  waiting for transfers between devices  94.6 us (43%)
  Pallas kernels  19.9 us (9%)
  local copies, waits for them, and re-layouts  4.97 us (2%)
  other arithmetic  4.35 us (2%)
    ppermute x11, waiting for transfers between devices, shift(): return lax.ppermute(value, axis, [(i, (i + step) % n) for i in range(n)])  89.3 us
    ppermute x11, starting transfers between devices, shift(): return lax.ppermute(value, axis, [(i, (i + step) % n) for i in range(n)])  39.9 us
    all_to_all x1, starting transfers between devices, shards(): lax.all_to_all(packed, ('zhi', 'x'), split_axis=0, concat_axis=0, tiled=T...  30.4 us
    pallas_call x2, Pallas kernels, local_call(): pl.pallas_call(kernel, out_shape=out_shape(packed), in_specs=[smem] * 3 +...  15.3 us
    ppermute x1, starting transfers between devices, fold_far(): came = lax.ppermute(away.astype(LOW), axis, [(i, i ^ 1) for i in range(4)])  13.4 us
    ppermute x1, starting transfers between devices, fold_far(): back = lax.ppermute(other.astype(LOW), axis, [(i, 3 - i) for i in range(4)])  10.9 us
  transfers between devices with their start and end apart: 14, of which 11 were waited for; matrix products, arithmetic and copies ran while one was open for 2% of the time, Pallas kernels for 4%

profile of v2, /device:TPU:46, one launch (start us, length us, event | category | flops | bytes accessed | tf_op | source)
XLA Modules:
  0.0 219.4 jit_solution(15868274188284475096)
XLA Ops:
  0.6 7.8 %shard_map.102 = bf16[640,512]{1,0:T(8,128)(2,1)} custom-call(s32[1]{0:T(128)} %bitcast.index_ref, s32[16,16]{1,0:T(8,128)} %lengths_ref.3, s32[16,16]{1,0:T(8,128)} %plan_ref.3, bf16[512,512]{1,0:T(8,128)(2,1)} %bitcast.67, bf16[512,128]{1,0:T(8,128)(2,1)} %bitcast.74, bf16[512,128]{1,0:T(8,128)(2,1)} %bitcast.73, bf16[512,512]{1,0:T(8,128)(2,1)} %bitcast.69), custom_call_target="tpu_custom_call" | custom-call | flops 2000000000 | bytes 1310720 | tf_op jit(solution)/shard_map/pallas_call | solution.py:209
  8.5 30.4 %all-to-all-start = ((bf16[16,40,512]{2,1,0:T(8,128)(2,1)}), bf16[16,40,512]{2,1,0:T(8,128)(2,1)S(1)}, u32[]{:S(2)}, u32[]{:S(2)}) async-start(bf16[16,40,512]{2,1,0:T(8,128)(2,1)} %bitcast.65), calls=%async_computation | async-start | bytes 1310720 | tf_op jit(solution)/shard_map/all_to_all | solution.py:346
  38.9 7.5 %shard_map.103 = bf16[512,128]{1,0:T(8,128)(2,1)} custom-call(s32[1]{0:T(128)} %bitcast.index_ref, s32[16,16]{1,0:T(8,128)} %lengths_ref.3, s32[16,16]{1,0:T(8,128)} %plan_ref.3, bf16[512,512]{1,0:T(8,128)(2,1)} %bitcast.68, bf16[512,128]{1,0:T(8,128)(2,1)} %bitcast.75, bf16[512,512]{1,0:T(8,128)(2,1)} %bitcast.70), custom_call_target="tpu_custom_call" | custom-call | flops 1000000000 | bytes 1179648 | tf_op jit(solution)/shard_map/pallas_call | solution.py:209
  46.4 4.3 %collective-permute-start = (bf16[512,128]{1,0:T(8,128)(2,1)}, bf16[512,128]{1,0:T(8,128)(2,1)S(1)}, u32[]{:S(2)}, u32[]{:S(2)}) collective-permute-start(bf16[512,128]{1,0:T(8,128)(2,1)} %shard_map.103), channel_id=1, source_target_pairs={{0,4},{4,0},{1,5},{5,1},{2,6},{6,2},{3,7},{7,3},{8,12},{12,8},{9,1... | collective-permute-start | bytes 393224 | tf_op jit(solution)/shard_map/ppermute | solution.py:307
  50.7 53.4 %collective-permute-done = bf16[512,128]{1,0:T(8,128)(2,1)S(1)} collective-permute-done((bf16[512,128]{1,0:T(8,128)(2,1)}, bf16[512,128]{1,0:T(8,128)(2,1)S(1)}, u32[]{:S(2)}, u32[]{:S(2)}) %collective-permute-start) | collective-permute-done | bytes 131104 | tf_op jit(solution)/shard_map/ppermute | solution.py:307
  106.9 10.0 %collective-permute-start.2 = (bf16[512,256]{1,0:T(8,128)(2,1)S(1)}, bf16[512,256]{1,0:T(8,128)(2,1)S(1)}, u32[]{:S(2)}, u32[]{:S(2)}) collective-permute-start(bf16[512,256]{1,0:T(8,128)(2,1)S(1)} %pad_maximum_fusion.refs_0_), channel_id=1, source_target_pairs={{0,2},{1,3},{2,0},{3,1},{4,6},{5,7},{6,4},{7,5},{8,10},{9,11},{10,... | collective-permute-start | bytes 786440 | tf_op jit(solution)/shard_map/ppermute | solution.py:307
  117.0 1.9 collective-permute-start.3
  120.3 12.0 %collective-permute-done.2.refs_2_ = bf16[512,256]{1,0:T(8,128)(2,1)S(1)} collective-permute-done((bf16[512,256]{1,0:T(8,128)(2,1)S(1)}, bf16[512,256]{1,0:T(8,128)(2,1)S(1)}, u32[]{:S(2)}, u32[]{:S(2)}) %collective-permute-start.2) | collective-permute-done | bytes 262176 | tf_op jit(solution)/shard_map/ppermute | solution.py:307
  132.3 4.2 %collective-permute-done.3.refs_3_ = bf16[512,256]{1,0:T(8,128)(2,1)S(1)} collective-permute-done((bf16[512,256]{1,0:T(8,128)(2,1)S(1)}, bf16[512,256]{1,0:T(8,128)(2,1)S(1)}, u32[]{:S(2)}, u32[]{:S(2)}) %collective-permute-start.3) | collective-permute-done | bytes 262176 | tf_op jit(solution)/shard_map/ppermute | solution.py:307
  141.3 1.9 collective-permute-start.4
  143.2 2.9 %collective-permute-done.4 = bf16[512,1024]{1,0:T(8,128)(2,1)} collective-permute-done((bf16[512,1024]{1,0:T(8,128)(2,1)}, bf16[512,1024]{1,0:T(8,128)(2,1)}, u32[]{:S(2)}, u32[]{:S(2)}) %collective-permute-start.4) | collective-permute-done | bytes 1048608 | tf_op jit(solution)/shard_map/ppermute | solution.py:307
  149.1 3.5 %collective-permute-start.5 = (bf16[4,4,8,1024]{3,2,1,0:T(8,128)(2,1)S(1)}, bf16[4,4,8,1024]{3,2,1,0:T(8,128)(2,1)S(1)}, u32[]{:S(2)}, u32[]{:S(2)}) collective-permute-start(bf16[4,4,8,1024]{3,2,1,0:T(8,128)(2,1)S(1)} %get-tuple-element.14), channel_id=1, source_target_pairs={{0,256},{256,512},{512,768},{768,0},{1,257},{257,513},{513,769},{7... | collective-permute-start | bytes 786440 | tf_op jit(solution)/shard_map/ppermute | solution.py:307
  152.6 2.9 %collective-permute-start.6 = (bf16[4,4,8,1024]{3,2,1,0:T(8,128)(2,1)S(1)}, bf16[4,4,8,1024]{3,2,1,0:T(8,128)(2,1)S(1)}, u32[]{:S(2)}, u32[]{:S(2)}) collective-permute-start(bf16[4,4,8,1024]{3,2,1,0:T(8,128)(2,1)S(1)} %get-tuple-element.16), channel_id=1, source_target_pairs={{0,512},{256,768},{512,0},{768,256},{1,513},{257,769},{513,1},{769... | collective-permute-start | bytes 786440 | tf_op jit(solution)/shard_map/ppermute | solution.py:307
  155.5 4.3 %collective-permute-start.7 = (bf16[4,4,8,1024]{3,2,1,0:T(8,128)(2,1)S(1)}, bf16[4,4,8,1024]{3,2,1,0:T(8,128)(2,1)S(1)}, u32[]{:S(2)}, u32[]{:S(2)}) collective-permute-start(bf16[4,4,8,1024]{3,2,1,0:T(8,128)(2,1)S(1)} %get-tuple-element.15), channel_id=1, source_target_pairs={{0,768},{256,0},{512,256},{768,512},{1,769},{257,1},{513,257},{769... | collective-permute-start | bytes 786440 | tf_op jit(solution)/shard_map/ppermute | solution.py:307
  160.2 5.0 %collective-permute-done.6 = bf16[4,4,8,1024]{3,2,1,0:T(8,128)(2,1)S(1)} collective-permute-done((bf16[4,4,8,1024]{3,2,1,0:T(8,128)(2,1)S(1)}, bf16[4,4,8,1024]{3,2,1,0:T(8,128)(2,1)S(1)}, u32[]{:S(2)}, u32[]{:S(2)}) %collective-permute-start.6) | collective-permute-done | bytes 262176 | tf_op jit(solution)/shard_map/ppermute | solution.py:307
  165.3 4.5 %collective-permute-done.7 = bf16[4,4,8,1024]{3,2,1,0:T(8,128)(2,1)S(1)} collective-permute-done((bf16[4,4,8,1024]{3,2,1,0:T(8,128)(2,1)S(1)}, bf16[4,4,8,1024]{3,2,1,0:T(8,128)(2,1)S(1)}, u32[]{:S(2)}, u32[]{:S(2)}) %collective-permute-start.7) | collective-permute-done | bytes 262176 | tf_op jit(solution)/shard_map/ppermute | solution.py:307
  170.9 2.8 %collective-permute-start.10 = (bf16[4,8,1024]{2,1,0:T(8,128)(2,1)S(1)}, bf16[4,8,1024]{2,1,0:T(8,128)(2,1)S(1)}, u32[]{:S(2)}, u32[]{:S(2)}) collective-permute-start(bf16[4,8,1024]{2,1,0:T(8,128)(2,1)S(1)} %get-tuple-element.18), channel_id=1, source_target_pairs={{0,24},{8,0},{16,8},{24,16},{1,25},{9,1},{17,9},{25,17},{2,26},{10... | collective-permute-start | bytes 196616 | tf_op jit(solution)/shard_map/ppermute | solution.py:307
  173.7 4.3 %collective-permute-start.8 = (bf16[4,8,1024]{2,1,0:T(8,128)(2,1)S(1)}, bf16[4,8,1024]{2,1,0:T(8,128)(2,1)S(1)}, u32[]{:S(2)}, u32[]{:S(2)}) collective-permute-start(bf16[4,8,1024]{2,1,0:T(8,128)(2,1)S(1)} %get-tuple-element.17), channel_id=1, source_target_pairs={{0,8},{8,16},{16,24},{24,0},{1,9},{9,17},{17,25},{25,1},{2,10},{10... | collective-permute-start | bytes 196616 | tf_op jit(solution)/shard_map/ppermute | solution.py:307
  178.0 2.2 collective-permute-start.9
  180.3 5.4 %collective-permute-done.9 = bf16[4,8,1024]{2,1,0:T(8,128)(2,1)S(1)} collective-permute-done((bf16[4,8,1024]{2,1,0:T(8,128)(2,1)S(1)}, bf16[4,8,1024]{2,1,0:T(8,128)(2,1)S(1)}, u32[]{:S(2)}, u32[]{:S(2)}) %collective-permute-start.9) | collective-permute-done | bytes 65568 | tf_op jit(solution)/shard_map/ppermute | solution.py:307
  185.7 13.4 %collective-permute-start.11 = (bf16[2,8,1024]{2,1,0:T(8,128)(2,1)S(1)}, bf16[2,8,1024]{2,1,0:T(8,128)(2,1)S(1)}, u32[]{:S(2)}, u32[]{:S(2)}) collective-permute-start(bf16[2,8,1024]{2,1,0:T(8,128)(2,1)S(1)} %pad_maximum_fusion.1), channel_id=1, source_target_pairs={{0,32},{32,0},{64,96},{96,64},{1,33},{33,1},{65,97},{97,65},{2,34}... | collective-permute-start | bytes 98312 | tf_op jit(solution)/shard_map/ppermute | solution.py:328
  201.1 10.9 %collective-permute-start.12 = (bf16[8,1024]{1,0:T(8,128)(2,1)S(1)}, bf16[8,1024]{1,0:T(8,128)(2,1)S(1)}, u32[]{:S(2)}, u32[]{:S(2)}) collective-permute-start(bf16[8,1024]{1,0:T(8,128)(2,1)S(1)} %fusion.11), channel_id=1, source_target_pairs={{0,96},{32,64},{64,32},{96,0},{1,97},{33,65},{65,33},{97,1},{2,98}... | collective-permute-start | bytes 49160 | tf_op jit(solution)/shard_map/ppermute | solution.py:331
  212.0 3.4 %collective-permute-done.12 = bf16[8,1024]{1,0:T(8,128)(2,1)S(1)} collective-permute-done((bf16[8,1024]{1,0:T(8,128)(2,1)S(1)}, bf16[8,1024]{1,0:T(8,128)(2,1)S(1)}, u32[]{:S(2)}, u32[]{:S(2)}) %collective-permute-start.12) | collective-permute-done | bytes 16416 | tf_op jit(solution)/shard_map/ppermute | solution.py:331
  216.6 2.7 %finish.1 = (bf16[640,512]{1,0:T(8,128)(2,1)}, bf16[640,128]{1,0:T(8,128)(2,1)}, bf16[640,128]{1,0:T(8,128)(2,1)}) custom-call(bf16[640,512]{1,0:T(8,128)(2,1)S(1)} %bitcast.61), custom_call_target="tpu_custom_call" | custom-call | tf_op jit(solution)/shard_map/finish/pallas_call | solution.py:264
  (32 shorter events, 16.7 us)
Async XLA Ops:
  8.5 208.1 %all-to-all-start = ((bf16[16,40,512]{2,1,0:T(8,128)(2,1)}), bf16[16,40,512]{2,1,0:T(8,128)(2,1)S(1)}, u32[]{:S(2)}, u32[]{:S(2)}) async-start(bf16[16,40,512]{2,1,0:T(8,128)(2,1)} %bitcast.65), calls=%async_computation | async-start | bytes 1310720 | tf_op jit(solution)/shard_map/all_to_all | solution.py:346
  46.4 57.7 %collective-permute-start = (bf16[512,128]{1,0:T(8,128)(2,1)}, bf16[512,128]{1,0:T(8,128)(2,1)S(1)}, u32[]{:S(2)}, u32[]{:S(2)}) collective-permute-start(bf16[512,128]{1,0:T(8,128)(2,1)} %shard_map.103), channel_id=1, source_target_pairs={{0,4},{4,0},{1,5},{5,1},{2,6},{6,2},{3,7},{7,3},{8,12},{12,8},{9,1... | collective-permute-start | bytes 393224 | tf_op jit(solution)/shard_map/ppermute | solution.py:307
  105.0 15.3 %collective-permute-start.1 = (bf16[512,256]{1,0:T(8,128)(2,1)S(1)}, bf16[512,256]{1,0:T(8,128)(2,1)S(1)}, u32[]{:S(2)}, u32[]{:S(2)}) collective-permute-start(bf16[512,256]{1,0:T(8,128)(2,1)S(1)} %pad_maximum_fusion.refs_0_), channel_id=1, source_target_pairs={{0,1},{1,2},{2,3},{3,0},{4,5},{5,6},{6,7},{7,4},{8,9},{9,10},{10,1... | collective-permute-start | bytes 786440 | tf_op jit(solution)/shard_map/ppermute | solution.py:307
  106.9 25.4 %collective-permute-start.2 = (bf16[512,256]{1,0:T(8,128)(2,1)S(1)}, bf16[512,256]{1,0:T(8,128)(2,1)S(1)}, u32[]{:S(2)}, u32[]{:S(2)}) collective-permute-start(bf16[512,256]{1,0:T(8,128)(2,1)S(1)} %pad_maximum_fusion.refs_0_), channel_id=1, source_target_pairs={{0,2},{1,3},{2,0},{3,1},{4,6},{5,7},{6,4},{7,5},{8,10},{9,11},{10,... | collective-permute-start | bytes 786440 | tf_op jit(solution)/shard_map/ppermute | solution.py:307
  117.0 19.6 %collective-permute-start.3 = (bf16[512,256]{1,0:T(8,128)(2,1)S(1)}, bf16[512,256]{1,0:T(8,128)(2,1)S(1)}, u32[]{:S(2)}, u32[]{:S(2)}) collective-permute-start(bf16[512,256]{1,0:T(8,128)(2,1)S(1)} %pad_maximum_fusion.refs_0_), channel_id=1, source_target_pairs={{0,3},{1,0},{2,1},{3,2},{4,7},{5,4},{6,5},{7,6},{8,11},{9,8},{10,9... | collective-permute-start | bytes 786440 | tf_op jit(solution)/shard_map/ppermute | solution.py:307
  136.5 0.7 copy-start.1
  137.2 1.2 copy-start
  138.5 0.9 copy-start.2
  141.3 4.9 %collective-permute-start.4 = (bf16[512,1024]{1,0:T(8,128)(2,1)}, bf16[512,1024]{1,0:T(8,128)(2,1)}, u32[]{:S(2)}, u32[]{:S(2)}) collective-permute-start(bf16[512,1024]{1,0:T(8,128)(2,1)} %get-tuple-element.13), channel_id=1, source_target_pairs={{0,128},{128,0},{1,129},{129,1},{2,130},{130,2},{3,131},{131,3},{4... | collective-permute-start | bytes 3145736 | tf_op jit(solution)/shard_map/ppermute | solution.py:307
  147.7 1.3 copy-start.3
  149.1 11.1 %collective-permute-start.5 = (bf16[4,4,8,1024]{3,2,1,0:T(8,128)(2,1)S(1)}, bf16[4,4,8,1024]{3,2,1,0:T(8,128)(2,1)S(1)}, u32[]{:S(2)}, u32[]{:S(2)}) collective-permute-start(bf16[4,4,8,1024]{3,2,1,0:T(8,128)(2,1)S(1)} %get-tuple-element.14), channel_id=1, source_target_pairs={{0,256},{256,512},{512,768},{768,0},{1,257},{257,513},{513,769},{7... | collective-permute-start | bytes 786440 | tf_op jit(solution)/shard_map/ppermute | solution.py:307
  152.6 12.6 %collective-permute-start.6 = (bf16[4,4,8,1024]{3,2,1,0:T(8,128)(2,1)S(1)}, bf16[4,4,8,1024]{3,2,1,0:T(8,128)(2,1)S(1)}, u32[]{:S(2)}, u32[]{:S(2)}) collective-permute-start(bf16[4,4,8,1024]{3,2,1,0:T(8,128)(2,1)S(1)} %get-tuple-element.16), channel_id=1, source_target_pairs={{0,512},{256,768},{512,0},{768,256},{1,513},{257,769},{513,1},{769... | collective-permute-start | bytes 786440 | tf_op jit(solution)/shard_map/ppermute | solution.py:307
  155.5 14.2 %collective-permute-start.7 = (bf16[4,4,8,1024]{3,2,1,0:T(8,128)(2,1)S(1)}, bf16[4,4,8,1024]{3,2,1,0:T(8,128)(2,1)S(1)}, u32[]{:S(2)}, u32[]{:S(2)}) collective-permute-start(bf16[4,4,8,1024]{3,2,1,0:T(8,128)(2,1)S(1)} %get-tuple-element.15), channel_id=1, source_target_pairs={{0,768},{256,0},{512,256},{768,512},{1,769},{257,1},{513,257},{769... | collective-permute-start | bytes 786440 | tf_op jit(solution)/shard_map/ppermute | solution.py:307
  170.9 9.3 %collective-permute-start.10 = (bf16[4,8,1024]{2,1,0:T(8,128)(2,1)S(1)}, bf16[4,8,1024]{2,1,0:T(8,128)(2,1)S(1)}, u32[]{:S(2)}, u32[]{:S(2)}) collective-permute-start(bf16[4,8,1024]{2,1,0:T(8,128)(2,1)S(1)} %get-tuple-element.18), channel_id=1, source_target_pairs={{0,24},{8,0},{16,8},{24,16},{1,25},{9,1},{17,9},{25,17},{2,26},{10... | collective-permute-start | bytes 196616 | tf_op jit(solution)/shard_map/ppermute | solution.py:307
  173.7 6.5 %collective-permute-start.8 = (bf16[4,8,1024]{2,1,0:T(8,128)(2,1)S(1)}, bf16[4,8,1024]{2,1,0:T(8,128)(2,1)S(1)}, u32[]{:S(2)}, u32[]{:S(2)}) collective-permute-start(bf16[4,8,1024]{2,1,0:T(8,128)(2,1)S(1)} %get-tuple-element.17), channel_id=1, source_target_pairs={{0,8},{8,16},{16,24},{24,0},{1,9},{9,17},{17,25},{25,1},{2,10},{10... | collective-permute-start | bytes 196616 | tf_op jit(solution)/shard_map/ppermute | solution.py:307
  178.0 7.7 %collective-permute-start.9 = (bf16[4,8,1024]{2,1,0:T(8,128)(2,1)S(1)}, bf16[4,8,1024]{2,1,0:T(8,128)(2,1)S(1)}, u32[]{:S(2)}, u32[]{:S(2)}) collective-permute-start(bf16[4,8,1024]{2,1,0:T(8,128)(2,1)S(1)} %get-tuple-element.19), channel_id=1, source_target_pairs={{0,16},{8,24},{16,0},{24,8},{1,17},{9,25},{17,1},{25,9},{2,18},{10... | collective-permute-start | bytes 196616 | tf_op jit(solution)/shard_map/ppermute | solution.py:307
  185.7 15.3 %collective-permute-start.11 = (bf16[2,8,1024]{2,1,0:T(8,128)(2,1)S(1)}, bf16[2,8,1024]{2,1,0:T(8,128)(2,1)S(1)}, u32[]{:S(2)}, u32[]{:S(2)}) collective-permute-start(bf16[2,8,1024]{2,1,0:T(8,128)(2,1)S(1)} %pad_maximum_fusion.1), channel_id=1, source_target_pairs={{0,32},{32,0},{64,96},{96,64},{1,33},{33,1},{65,97},{97,65},{2,34}... | collective-permute-start | bytes 98312 | tf_op jit(solution)/shard_map/ppermute | solution.py:328
  201.1 14.3 %collective-permute-start.12 = (bf16[8,1024]{1,0:T(8,128)(2,1)S(1)}, bf16[8,1024]{1,0:T(8,128)(2,1)S(1)}, u32[]{:S(2)}, u32[]{:S(2)}) collective-permute-start(bf16[8,1024]{1,0:T(8,128)(2,1)S(1)} %fusion.11), channel_id=1, source_target_pairs={{0,96},{32,64},{64,32},{96,0},{1,97},{33,65},{65,33},{97,1},{2,98}... | collective-permute-start | bytes 49160 | tf_op jit(solution)/shard_map/ppermute | solution.py:331

commit v3 on v2

--- a/solution.py
+++ b/solution.py
@@ -122,26 +122,31 @@
     query_ref,
     key_ref,
     grad_ref,
-    place_ref,
+    sums_ref,
     sems,
 ):
     copies = fetch(((query_hbm, query_ref), (key_hbm, key_ref), (grad_hbm, grad_ref)), sems)
-    seq_len = query_ref.shape[0]
-    capacity = place_ref.shape[0] // lengths_ref.shape[1]
-    tile = DOCS * capacity
-    place_rows(index_ref, lengths_ref, plan_ref, place_ref, capacity)
-    bias = softmax_bias(capacity)
+    own = index_ref[0]
+    starts = [jnp.int32(0)]
+    for d in range(lengths_ref.shape[1] - 1):
+        starts.append(starts[-1] + lengths_ref[own, d])
+    sums_ref[...] = jnp.zeros_like(sums_ref)
     for copy in copies:
         copy.wait()
-    sums = jnp.zeros(tokens_ref.shape, jnp.float32)
-    for part in range(place_ref.shape[0] // tile):
-        pick = picker(place_ref, slice(part * tile, (part + 1) * tile), seq_len)
-        query = by_head(dot(pick, query_ref[...]).astype(LOW))
-        grad = by_head(dot(pick, grad_ref[...]).astype(LOW))
-        key = dot(pick, key_ref[...]).astype(LOW)
-        probs_low = softmax(query, key, bias).astype(LOW)
-        sums += tn_dot(pick, tn_dot(probs_low, grad).astype(LOW))
-    tokens_ref[...] = sums.astype(LOW)
+    for tile in range(query_ref.shape[0] // HD):
+        here = slice(tile * HD, (tile + 1) * HD)
+        left = max(tile - 1, 0) * HD
+        window = slice(left, (tile + 1) * HD)
+        rows, cols = iotas(HD, here.stop - left)
+        rows, cols = rows + here.start, cols + left
+        first = jnp.zeros_like(rows)
+        for start in starts[1:]:
+            first = jnp.where(rows >= start, start, first)
+        bias = jnp.where((cols <= rows) & (cols >= first), 0.0, NEG)
+        bias = jnp.concatenate([bias] * GROUP, axis=0)
+        probs = softmax(by_head(query_ref[here, :]), key_ref[window, :], bias)
+        sums_ref[window, :] += tn_dot(probs.astype(LOW), by_head(grad_ref[here, :]))
+    tokens_ref[...] = sums_ref[...].astype(LOW)
 
 
 def attend_kernel(
@@ -200,7 +205,7 @@
         packed_ref[here, 3 * HD : 4 * HD] = (below + dot(flip, above)).astype(LOW)
 
 
-def local_call(kernel, plan_of, arrays, out_shape, flops):
+def local_call(kernel, plan_of, arrays, out_shape, scratch, flops):
     seq_len = arrays[0].shape[0]
     docs = plan_of[1].shape[1]
     packed = docs * (5 * seq_len // (4 * docs))
@@ -212,7 +217,7 @@
         in_specs=[smem] * 3 + [pl.BlockSpec(memory_space=pl.ANY)] * len(arrays),
         out_specs=pl.BlockSpec(memory_space=pltpu.VMEM),
         scratch_shapes=[pltpu.VMEM(a.shape, LOW) for a in arrays]
-        + [pltpu.VMEM((packed, HD), jnp.int32), pltpu.SemaphoreType.DMA((len(arrays),))],
+        + [scratch(packed), pltpu.SemaphoreType.DMA((len(arrays),))],
         compiler_params=pltpu.CompilerParams(vmem_limit_bytes=60 << 20),
         cost_estimate=pl.CostEstimate(flops=flops, bytes_accessed=moved, transcendentals=400000),
     )(*plan_of, *arrays)
@@ -224,6 +229,7 @@
         plan_of,
         (query, key, grad),
         lambda packed: jax.ShapeDtypeStruct(key.shape, LOW),
+        lambda packed: pltpu.VMEM(key.shape, jnp.float32),
         10**9,
     )
 
@@ -234,6 +240,7 @@
         plan_of,
         (query, key, value, grad),
         lambda packed: jax.ShapeDtypeStruct((packed, 4 * HD), LOW),
+        lambda packed: pltpu.VMEM((packed, HD), jnp.int32),
         2 * 10**9,
     )
 
@@ -307,29 +314,62 @@
     return lax.ppermute(value, axis, [(i, (i + step) % n) for i in range(n)])
 
 
-def fold(total, axis, dim):
+def pieces_kernel(choose, me_ref, own_ref, *refs):
+    *others, total_ref = refs
+    total = own_ref[...]
+    picks = choose(me_ref[0])
+    for came in others[: len(others) - len(picks)]:
+        total = total + came[...].astype(jnp.float32)
+    total_ref[...] = total
+    for out_ref, blocks in zip(others[len(others) - len(picks) :], picks):
+        size = out_ref.shape[0] // len(blocks)
+        parts = [total_ref[pl.ds(pl.multiple_of(b * size, 8), size), :] for b in blocks]
+        out_ref[...] = jnp.concatenate(parts, axis=0).astype(out_ref.dtype)
+
+
+def pieces(axis, own, came, choose, shares):
+    me = lax.axis_index(axis).astype(jnp.int32).reshape(1)
+    rows, width = own.shape
+    vmem = pl.BlockSpec(memory_space=pltpu.VMEM)
+    return pl.pallas_call(
+        functools.partial(pieces_kernel, choose),
+        out_shape=tuple(
+            jax.ShapeDtypeStruct((rows * of // total, width), dtype) for of, total, dtype in shares
+        ),
+        in_specs=[pl.BlockSpec(memory_space=pltpu.SMEM)] + [vmem] * (1 + len(came)),
+        out_specs=(vmem,) * len(shares),
+        scratch_shapes=[pltpu.VMEM((rows, width), jnp.float32)],
+        compiler_params=pltpu.CompilerParams(vmem_limit_bytes=24 << 20),
+        name="pieces",
+    )(me, own, *came)
+
+
+def exchange(axis, own, came, outer):
     n = lax.axis_size(axis)
-    me = lax.axis_index(axis)
-    summed = lax.dynamic_index_in_dim(total, me, dim, keepdims=False)
+
+    def choose(me):
+        return [[z * n + lax.rem(me + step, n) for z in range(outer)] for step in range(n)]
+
+    shares = [(1, n, jnp.float32)] + [(1, n, LOW)] * (n - 1)
+    own, *parts = pieces(axis, own, came, choose, shares)
+    got = []
     for step in range(1, n):
-        piece = lax.dynamic_index_in_dim(total, lax.rem(me + step, n), dim, keepdims=False)
-        summed = summed + shift(piece.astype(LOW), axis, step).astype(jnp.float32)
-    return summed
-
-
-def fold_far(total, axis):
-    me = lax.axis_index(axis)
-    first, second = jnp.bitwise_xor(me, 1), 3 - me
-
-    def at(value, i):
-        return lax.dynamic_index_in_dim(value, i, 0, keepdims=False)
-
-    away = jnp.stack([at(total, first), at(total, 3 - first)])
-    came = lax.ppermute(away.astype(LOW), axis, [(i, i ^ 1) for i in range(4)])
-    mine = at(total, me) + came[0].astype(jnp.float32)
-    other = at(total, second) + came[1].astype(jnp.float32)
-    back = lax.ppermute(other.astype(LOW), axis, [(i, 3 - i) for i in range(4)])
-    return mine + back.astype(jnp.float32)
+        got.append(shift(parts[step - 1], axis, step))
+    return own, got
+
+
+def exchange_far(axis, own, came):
+    def choose(me):
+        first = jnp.bitwise_xor(me, 1)
+        return [[first, 3 - first], [me], [3 - me]]
+
+    shares = [(2, 4, LOW), (1, 4, jnp.float32), (1, 4, jnp.float32)]
+    away, mine, other = pieces(axis, own, came, choose, shares)
+    got = lax.ppermute(away, axis, [(i, i ^ 1) for i in range(4)]).astype(jnp.float32)
+    size = mine.shape[0]
+    back = (other + got[size:]).astype(LOW)
+    back = lax.ppermute(back, axis, [(i, 3 - i) for i in range(4)])
+    return mine + got[:size] + back.astype(jnp.float32)
 
 
 def shards(queries, key_rows, value_rows, out_grad, inputs, doc_lengths, doc_plan):
@@ -344,21 +384,17 @@
     for k in range(1, near):
         blocks += [shift(pair, "zr", k)]
     received = lax.all_to_all(packed, ("zhi", "x"), split_axis=0, concat_axis=0, tiled=True)
-    features, width = inputs.shape[2], sum(b.shape[1] for b in blocks)
-    ny, nc, nz, nx = (lax.axis_size(a) for a in ("y", "core", "zhi", "x"))
     core = lax.axis_index("core").astype(jnp.int32).reshape(1)
-    away, kept = terms(core, inputs[0], blocks, nc)
+    away, kept = terms(core, inputs[0], blocks, lax.axis_size("core"))
     came = shift(away, "core", 1)
-    total = kept + came.astype(jnp.float32)
-    total = total.reshape(ny, nz, nx, features // (ny * nc * nz * nx), width)
-    total = fold(total, "y", 0)
-    total = fold(total, "x", 1)
-    total = fold_far(total, "zhi")
+    own_sum, got = exchange("y", kept, [came], 1)
+    own_sum, got = exchange("x", own_sum, got, lax.axis_size("zhi"))
+    total = exchange_far("zhi", own_sum, got)
     total = total.reshape(-1, 2 * near, HD)
     zq, zr = lax.axis_index("zq"), lax.axis_index("zr")
     block = jnp.arange(2 * near)
     source = 2 * jnp.bitwise_and(zr - block, near - 1) + (block // near != zq)
-    total = jnp.take(total, source, axis=1).reshape(-1, width)
+    total = jnp.take(total, source, axis=1).reshape(total.shape[0], -1)
     query_grad, key_grad, value_grad = finish(received, packed.shape[0] // doc_plan.shape[1])
     return (query_grad[None], key_grad[None], value_grad[None], total)
 

time: 220 us -> 219 us (level)
  waiting for transfers between devices: 94.6 us -> 97.6 us
  other arithmetic: 4.35 us -> 1.61 us
    ppermute x11, waiting for transfers between devices: 89.3 us -> 92.3 us  [shift(): return lax.ppermute(value, axis, [(i, (i + step) % n) for i in range(n)])]
    pallas_call x2, Pallas kernels: 15.3 us -> 12.4 us  [local_call(): pl.pallas_call(kernel, out_shape=out_shape(packed), in_specs=[smem] * 3 +...]
    add x3 -> x0, other arithmetic: 2.73 us -> none  [the longest x1 1.52 us: shards(): total = kept + came.astype(jnp.float32)]
    pallas_call x0 -> x3, Pallas kernels: none -> 2.66 us  [pieces(): pl.pallas_call(functools.partial(pieces_kernel, choose), out_shape=tuple(...]
  transfers between devices with their start and end apart: 14 -> 14, of which waited for: 11 -> 11; matrix products, arithmetic and copies ran while one was open for 2% -> 1% of each run, Pallas kernels for 4% -> 4%
where the time goes in v3:
time: 219 us; the launch traced here: 218 us
  waiting for transfers between devices  97.6 us (45%)
  starting transfers between devices  94.8 us (43%)
  Pallas kernels  19.7 us (9%)
  local copies, waits for them, and re-layouts  3.5 us (2%)
    ppermute x11, waiting for transfers between devices, shift(): return lax.ppermute(value, axis, [(i, (i + step) % n) for i in range(n)])  92.3 us
    ppermute x11, starting transfers between devices, shift(): return lax.ppermute(value, axis, [(i, (i + step) % n) for i in range(n)])  40.1 us
    all_to_all x1, starting transfers between devices, shards(): lax.all_to_all(packed, ('zhi', 'x'), split_axis=0, concat_axis=0, tiled=T...  30.4 us
    ppermute x1, starting transfers between devices, exchange_far(): lax.ppermute(away, axis, [(i, i ^ 1) for i in range(4)]).astype(jnp.float32)  13.4 us
    pallas_call x2, Pallas kernels, local_call(): pl.pallas_call(kernel, out_shape=out_shape(packed), in_specs=[smem] * 3 +...  12.4 us
    ppermute x1, starting transfers between devices, exchange_far(): back = lax.ppermute(back, axis, [(i, 3 - i) for i in range(4)])  10.9 us
  transfers between devices with their start and end apart: 14, of which 11 were waited for; matrix products, arithmetic and copies ran while one was open for 1% of the time, Pallas kernels for 4%

profile of v3, /device:TPU:46, one launch (start us, length us, event | category | flops | bytes accessed | tf_op | source)
XLA Modules:
  0.0 218.0 jit_solution(9113324393683780685)
XLA Ops:
  0.6 7.8 %shard_map.102 = bf16[640,512]{1,0:T(8,128)(2,1)} custom-call(s32[1]{0:T(128)} %bitcast.index_ref, s32[16,16]{1,0:T(8,128)} %lengths_ref.3, s32[16,16]{1,0:T(8,128)} %plan_ref.3, bf16[512,512]{1,0:T(8,128)(2,1)} %bitcast.29, bf16[512,128]{1,0:T(8,128)(2,1)} %bitcast.36, bf16[512,128]{1,0:T(8,128)(2,1)} %bitcast.35, bf16[512,512]{1,0:T(8,128)(2,1)} %bitcast.31), custom_call_target="tpu_custom_call" | custom-call | flops 2000000000 | bytes 1310720 | tf_op jit(solution)/shard_map/pallas_call | solution.py:214
  8.5 30.4 %all-to-all-start = ((bf16[16,40,512]{2,1,0:T(8,128)(2,1)}), bf16[16,40,512]{2,1,0:T(8,128)(2,1)S(1)}, u32[]{:S(2)}, u32[]{:S(2)}) async-start(bf16[16,40,512]{2,1,0:T(8,128)(2,1)} %bitcast.27), calls=%async_computation | async-start | bytes 1310720 | tf_op jit(solution)/shard_map/all_to_all | solution.py:386
  38.9 4.6 %shard_map.103 = bf16[512,128]{1,0:T(8,128)(2,1)} custom-call(s32[1]{0:T(128)} %bitcast.index_ref, s32[16,16]{1,0:T(8,128)} %lengths_ref.3, s32[16,16]{1,0:T(8,128)} %plan_ref.3, bf16[512,512]{1,0:T(8,128)(2,1)} %bitcast.30, bf16[512,128]{1,0:T(8,128)(2,1)} %bitcast.37, bf16[512,512]{1,0:T(8,128)(2,1)} %bitcast.32), custom_call_target="tpu_custom_call" | custom-call | flops 1000000000 | bytes 1179648 | tf_op jit(solution)/shard_map/pallas_call | solution.py:214
  43.5 4.3 %collective-permute-start = (bf16[512,128]{1,0:T(8,128)(2,1)}, bf16[512,128]{1,0:T(8,128)(2,1)S(1)}, u32[]{:S(2)}, u32[]{:S(2)}) collective-permute-start(bf16[512,128]{1,0:T(8,128)(2,1)} %shard_map.103), channel_id=1, source_target_pairs={{0,4},{4,0},{1,5},{5,1},{2,6},{6,2},{3,7},{7,3},{8,12},{12,8},{9,1... | collective-permute-start | bytes 393224 | tf_op jit(solution)/shard_map/ppermute | solution.py:314
  47.8 56.2 %collective-permute-done = bf16[512,128]{1,0:T(8,128)(2,1)S(1)} collective-permute-done((bf16[512,128]{1,0:T(8,128)(2,1)}, bf16[512,128]{1,0:T(8,128)(2,1)S(1)}, u32[]{:S(2)}, u32[]{:S(2)}) %collective-permute-start) | collective-permute-done | bytes 131104 | tf_op jit(solution)/shard_map/ppermute | solution.py:314
  106.8 10.2 %collective-permute-start.2 = (bf16[512,256]{1,0:T(8,128)(2,1)S(1)}, bf16[512,256]{1,0:T(8,128)(2,1)S(1)}, u32[]{:S(2)}, u32[]{:S(2)}) collective-permute-start(bf16[512,256]{1,0:T(8,128)(2,1)S(1)} %pad_maximum_fusion.refs_0_), channel_id=1, source_target_pairs={{0,2},{1,3},{2,0},{3,1},{4,6},{5,7},{6,4},{7,5},{8,10},{9,11},{10,... | collective-permute-start | bytes 786440 | tf_op jit(solution)/shard_map/ppermute | solution.py:314
  120.3 12.0 %collective-permute-done.2.refs_2_ = bf16[512,256]{1,0:T(8,128)(2,1)S(1)} collective-permute-done((bf16[512,256]{1,0:T(8,128)(2,1)S(1)}, bf16[512,256]{1,0:T(8,128)(2,1)S(1)}, u32[]{:S(2)}, u32[]{:S(2)}) %collective-permute-start.2) | collective-permute-done | bytes 262176 | tf_op jit(solution)/shard_map/ppermute | solution.py:314
  132.3 4.2 %collective-permute-done.3.refs_3_ = bf16[512,256]{1,0:T(8,128)(2,1)S(1)} collective-permute-done((bf16[512,256]{1,0:T(8,128)(2,1)S(1)}, bf16[512,256]{1,0:T(8,128)(2,1)S(1)}, u32[]{:S(2)}, u32[]{:S(2)}) %collective-permute-start.3) | collective-permute-done | bytes 262176 | tf_op jit(solution)/shard_map/ppermute | solution.py:314
  141.3 1.9 collective-permute-start.4
  143.2 2.9 %collective-permute-done.4.refs_0_ = bf16[512,1024]{1,0:T(8,128)(2,1)} collective-permute-done((bf16[512,1024]{1,0:T(8,128)(2,1)}, bf16[512,1024]{1,0:T(8,128)(2,1)}, u32[]{:S(2)}, u32[]{:S(2)}) %collective-permute-start.4) | collective-permute-done | bytes 1048608 | tf_op jit(solution)/shard_map/ppermute | solution.py:314
  146.2 2.4 %pieces.3 = (f32[128,1024]{1,0:T(8,128)S(1)}, bf16[128,1024]{1,0:T(8,128)(2,1)}, bf16[128,1024]{1,0:T(8,128)(2,1)}, bf16[128,1024]{1,0:T(8,128)(2,1)S(1)}) custom-call(s32[1]{0:T(128)} %bitcast.13.me_ref, f32[512,1024]{1,0:T(8,128)S(1)} %get-tuple-element.23.own_ref, bf16[512,1024]{1,0:T(8,128)(2,1)} %collective-permute-done.4.refs_0_), custom_call_target="tpu_custom_call" | custom-call | tf_op jit(solution)/shard_map/pieces/pallas_call | solution.py:334
  148.6 3.5 %collective-permute-start.5 = (bf16[128,1024]{1,0:T(8,128)(2,1)}, bf16[128,1024]{1,0:T(8,128)(2,1)S(1)}, u32[]{:S(2)}, u32[]{:S(2)}) collective-permute-start(bf16[128,1024]{1,0:T(8,128)(2,1)} %get-tuple-element.26), channel_id=1, source_target_pairs={{0,256},{256,512},{512,768},{768,0},{1,257},{257,513},{513,769},{7... | collective-permute-start | bytes 786440 | tf_op jit(solution)/shard_map/ppermute | solution.py:314
  152.1 2.8 %collective-permute-start.6 = (bf16[128,1024]{1,0:T(8,128)(2,1)}, bf16[128,1024]{1,0:T(8,128)(2,1)S(1)}, u32[]{:S(2)}, u32[]{:S(2)}) collective-permute-start(bf16[128,1024]{1,0:T(8,128)(2,1)} %get-tuple-element.27), channel_id=1, source_target_pairs={{0,512},{256,768},{512,0},{768,256},{1,513},{257,769},{513,1},{769... | collective-permute-start | bytes 786440 | tf_op jit(solution)/shard_map/ppermute | solution.py:314
  154.9 4.3 %collective-permute-start.7 = (bf16[128,1024]{1,0:T(8,128)(2,1)S(1)}, bf16[128,1024]{1,0:T(8,128)(2,1)S(1)}, u32[]{:S(2)}, u32[]{:S(2)}) collective-permute-start(bf16[128,1024]{1,0:T(8,128)(2,1)S(1)} %get-tuple-element.28), channel_id=1, source_target_pairs={{0,768},{256,0},{512,256},{768,512},{1,769},{257,1},{513,257},{769... | collective-permute-start | bytes 786440 | tf_op jit(solution)/shard_map/ppermute | solution.py:314
  159.9 5.0 %collective-permute-done.6.refs_1_ = bf16[128,1024]{1,0:T(8,128)(2,1)S(1)} collective-permute-done((bf16[128,1024]{1,0:T(8,128)(2,1)}, bf16[128,1024]{1,0:T(8,128)(2,1)S(1)}, u32[]{:S(2)}, u32[]{:S(2)}) %collective-permute-start.6) | collective-permute-done | bytes 262176 | tf_op jit(solution)/shard_map/ppermute | solution.py:314
  164.9 4.5 %collective-permute-done.7.refs_2_ = bf16[128,1024]{1,0:T(8,128)(2,1)S(1)} collective-permute-done((bf16[128,1024]{1,0:T(8,128)(2,1)S(1)}, bf16[128,1024]{1,0:T(8,128)(2,1)S(1)}, u32[]{:S(2)}, u32[]{:S(2)}) %collective-permute-start.7) | collective-permute-done | bytes 262176 | tf_op jit(solution)/shard_map/ppermute | solution.py:314
  169.6 2.8 %collective-permute-start.10 = (bf16[32,1024]{1,0:T(8,128)(2,1)S(1)}, bf16[32,1024]{1,0:T(8,128)(2,1)S(1)}, u32[]{:S(2)}, u32[]{:S(2)}) collective-permute-start(bf16[32,1024]{1,0:T(8,128)(2,1)S(1)} %get-tuple-element.32), channel_id=1, source_target_pairs={{0,24},{8,0},{16,8},{24,16},{1,25},{9,1},{17,9},{25,17},{2,26},{10... | collective-permute-start | bytes 196616 | tf_op jit(solution)/shard_map/ppermute | solution.py:314
  172.4 4.3 %collective-permute-start.8 = (bf16[32,1024]{1,0:T(8,128)(2,1)S(1)}, bf16[32,1024]{1,0:T(8,128)(2,1)S(1)}, u32[]{:S(2)}, u32[]{:S(2)}) collective-permute-start(bf16[32,1024]{1,0:T(8,128)(2,1)S(1)} %get-tuple-element.30), channel_id=1, source_target_pairs={{0,8},{8,16},{16,24},{24,0},{1,9},{9,17},{17,25},{25,1},{2,10},{10... | collective-permute-start | bytes 196616 | tf_op jit(solution)/shard_map/ppermute | solution.py:314
  176.6 2.2 collective-permute-start.9
  178.9 5.4 %collective-permute-done.9.refs_1_ = bf16[32,1024]{1,0:T(8,128)(2,1)S(1)} collective-permute-done((bf16[32,1024]{1,0:T(8,128)(2,1)S(1)}, bf16[32,1024]{1,0:T(8,128)(2,1)S(1)}, u32[]{:S(2)}, u32[]{:S(2)}) %collective-permute-start.9) | collective-permute-done | bytes 65568 | tf_op jit(solution)/shard_map/ppermute | solution.py:314
  184.4 13.4 %collective-permute-start.11 = (bf16[16,1024]{1,0:T(8,128)(2,1)S(1)}, bf16[16,1024]{1,0:T(8,128)(2,1)S(1)}, u32[]{:S(2)}, u32[]{:S(2)}) collective-permute-start(bf16[16,1024]{1,0:T(8,128)(2,1)S(1)} %get-tuple-element.34), channel_id=1, source_target_pairs={{0,32},{32,0},{64,96},{96,64},{1,33},{33,1},{65,97},{97,65},{2,34}... | collective-permute-start | bytes 98312 | tf_op jit(solution)/shard_map/ppermute | solution.py:368
  199.7 10.9 %collective-permute-start.12 = (bf16[8,1024]{1,0:T(8,128)(2,1)S(1)}, bf16[8,1024]{1,0:T(8,128)(2,1)S(1)}, u32[]{:S(2)}, u32[]{:S(2)}) collective-permute-start(bf16[8,1024]{1,0:T(8,128)(2,1)S(1)} %fusion), channel_id=1, source_target_pairs={{0,96},{32,64},{64,32},{96,0},{1,97},{33,65},{65,33},{97,1},{2,98}... | collective-permute-start | bytes 49160 | tf_op jit(solution)/shard_map/ppermute | solution.py:371
  210.6 3.4 %collective-permute-done.12 = bf16[8,1024]{1,0:T(8,128)(2,1)S(1)} collective-permute-done((bf16[8,1024]{1,0:T(8,128)(2,1)S(1)}, bf16[8,1024]{1,0:T(8,128)(2,1)S(1)}, u32[]{:S(2)}, u32[]{:S(2)}) %collective-permute-start.12) | collective-permute-done | bytes 16416 | tf_op jit(solution)/shard_map/ppermute | solution.py:371
  215.2 2.7 %finish.1 = (bf16[640,512]{1,0:T(8,128)(2,1)}, bf16[640,128]{1,0:T(8,128)(2,1)}, bf16[640,128]{1,0:T(8,128)(2,1)}) custom-call(bf16[640,512]{1,0:T(8,128)(2,1)S(1)} %bitcast.25), custom_call_target="tpu_custom_call" | custom-call | tf_op jit(solution)/shard_map/finish/pallas_call | solution.py:271
  (27 shorter events, 14.9 us)
Async XLA Ops:
  8.5 206.7 %all-to-all-start = ((bf16[16,40,512]{2,1,0:T(8,128)(2,1)}), bf16[16,40,512]{2,1,0:T(8,128)(2,1)S(1)}, u32[]{:S(2)}, u32[]{:S(2)}) async-start(bf16[16,40,512]{2,1,0:T(8,128)(2,1)} %bitcast.27), calls=%async_computation | async-start | bytes 1310720 | tf_op jit(solution)/shard_map/all_to_all | solution.py:386
  43.5 60.5 %collective-permute-start = (bf16[512,128]{1,0:T(8,128)(2,1)}, bf16[512,128]{1,0:T(8,128)(2,1)S(1)}, u32[]{:S(2)}, u32[]{:S(2)}) collective-permute-start(bf16[512,128]{1,0:T(8,128)(2,1)} %shard_map.103), channel_id=1, source_target_pairs={{0,4},{4,0},{1,5},{5,1},{2,6},{6,2},{3,7},{7,3},{8,12},{12,8},{9,1... | collective-permute-start | bytes 393224 | tf_op jit(solution)/shard_map/ppermute | solution.py:314
  104.9 15.4 %collective-permute-start.1 = (bf16[512,256]{1,0:T(8,128)(2,1)S(1)}, bf16[512,256]{1,0:T(8,128)(2,1)S(1)}, u32[]{:S(2)}, u32[]{:S(2)}) collective-permute-start(bf16[512,256]{1,0:T(8,128)(2,1)S(1)} %pad_maximum_fusion.refs_0_), channel_id=1, source_target_pairs={{0,1},{1,2},{2,3},{3,0},{4,5},{5,6},{6,7},{7,4},{8,9},{9,10},{10,1... | collective-permute-start | bytes 786440 | tf_op jit(solution)/shard_map/ppermute | solution.py:314
  106.8 25.5 %collective-permute-start.2 = (bf16[512,256]{1,0:T(8,128)(2,1)S(1)}, bf16[512,256]{1,0:T(8,128)(2,1)S(1)}, u32[]{:S(2)}, u32[]{:S(2)}) collective-permute-start(bf16[512,256]{1,0:T(8,128)(2,1)S(1)} %pad_maximum_fusion.refs_0_), channel_id=1, source_target_pairs={{0,2},{1,3},{2,0},{3,1},{4,6},{5,7},{6,4},{7,5},{8,10},{9,11},{10,... | collective-permute-start | bytes 786440 | tf_op jit(solution)/shard_map/ppermute | solution.py:314
  117.0 19.6 %collective-permute-start.3 = (bf16[512,256]{1,0:T(8,128)(2,1)S(1)}, bf16[512,256]{1,0:T(8,128)(2,1)S(1)}, u32[]{:S(2)}, u32[]{:S(2)}) collective-permute-start(bf16[512,256]{1,0:T(8,128)(2,1)S(1)} %pad_maximum_fusion.refs_0_), channel_id=1, source_target_pairs={{0,3},{1,0},{2,1},{3,2},{4,7},{5,4},{6,5},{7,6},{8,11},{9,8},{10,9... | collective-permute-start | bytes 786440 | tf_op jit(solution)/shard_map/ppermute | solution.py:314
  136.6 0.7 copy-start.1
  137.3 1.2 copy-start
  138.5 0.9 copy-start.2
  141.3 4.9 %collective-permute-start.4 = (bf16[512,1024]{1,0:T(8,128)(2,1)}, bf16[512,1024]{1,0:T(8,128)(2,1)}, u32[]{:S(2)}, u32[]{:S(2)}) collective-permute-start(bf16[512,1024]{1,0:T(8,128)(2,1)} %get-tuple-element.24), channel_id=1, source_target_pairs={{0,128},{128,0},{1,129},{129,1},{2,130},{130,2},{3,131},{131,3},{4... | collective-permute-start | bytes 3145736 | tf_op jit(solution)/shard_map/ppermute | solution.py:314
  148.6 11.3 %collective-permute-start.5 = (bf16[128,1024]{1,0:T(8,128)(2,1)}, bf16[128,1024]{1,0:T(8,128)(2,1)S(1)}, u32[]{:S(2)}, u32[]{:S(2)}) collective-permute-start(bf16[128,1024]{1,0:T(8,128)(2,1)} %get-tuple-element.26), channel_id=1, source_target_pairs={{0,256},{256,512},{512,768},{768,0},{1,257},{257,513},{513,769},{7... | collective-permute-start | bytes 786440 | tf_op jit(solution)/shard_map/ppermute | solution.py:314
  152.1 12.8 %collective-permute-start.6 = (bf16[128,1024]{1,0:T(8,128)(2,1)}, bf16[128,1024]{1,0:T(8,128)(2,1)S(1)}, u32[]{:S(2)}, u32[]{:S(2)}) collective-permute-start(bf16[128,1024]{1,0:T(8,128)(2,1)} %get-tuple-element.27), channel_id=1, source_target_pairs={{0,512},{256,768},{512,0},{768,256},{1,513},{257,769},{513,1},{769... | collective-permute-start | bytes 786440 | tf_op jit(solution)/shard_map/ppermute | solution.py:314
  154.9 14.4 %collective-permute-start.7 = (bf16[128,1024]{1,0:T(8,128)(2,1)S(1)}, bf16[128,1024]{1,0:T(8,128)(2,1)S(1)}, u32[]{:S(2)}, u32[]{:S(2)}) collective-permute-start(bf16[128,1024]{1,0:T(8,128)(2,1)S(1)} %get-tuple-element.28), channel_id=1, source_target_pairs={{0,768},{256,0},{512,256},{768,512},{1,769},{257,1},{513,257},{769... | collective-permute-start | bytes 786440 | tf_op jit(solution)/shard_map/ppermute | solution.py:314
  169.6 9.3 %collective-permute-start.10 = (bf16[32,1024]{1,0:T(8,128)(2,1)S(1)}, bf16[32,1024]{1,0:T(8,128)(2,1)S(1)}, u32[]{:S(2)}, u32[]{:S(2)}) collective-permute-start(bf16[32,1024]{1,0:T(8,128)(2,1)S(1)} %get-tuple-element.32), channel_id=1, source_target_pairs={{0,24},{8,0},{16,8},{24,16},{1,25},{9,1},{17,9},{25,17},{2,26},{10... | collective-permute-start | bytes 196616 | tf_op jit(solution)/shard_map/ppermute | solution.py:314
  172.4 6.5 %collective-permute-start.8 = (bf16[32,1024]{1,0:T(8,128)(2,1)S(1)}, bf16[32,1024]{1,0:T(8,128)(2,1)S(1)}, u32[]{:S(2)}, u32[]{:S(2)}) collective-permute-start(bf16[32,1024]{1,0:T(8,128)(2,1)S(1)} %get-tuple-element.30), channel_id=1, source_target_pairs={{0,8},{8,16},{16,24},{24,0},{1,9},{9,17},{17,25},{25,1},{2,10},{10... | collective-permute-start | bytes 196616 | tf_op jit(solution)/shard_map/ppermute | solution.py:314
  176.6 7.7 %collective-permute-start.9 = (bf16[32,1024]{1,0:T(8,128)(2,1)S(1)}, bf16[32,1024]{1,0:T(8,128)(2,1)S(1)}, u32[]{:S(2)}, u32[]{:S(2)}) collective-permute-start(bf16[32,1024]{1,0:T(8,128)(2,1)S(1)} %get-tuple-element.31), channel_id=1, source_target_pairs={{0,16},{8,24},{16,0},{24,8},{1,17},{9,25},{17,1},{25,9},{2,18},{10... | collective-permute-start | bytes 196616 | tf_op jit(solution)/shard_map/ppermute | solution.py:314
  184.4 15.3 %collective-permute-start.11 = (bf16[16,1024]{1,0:T(8,128)(2,1)S(1)}, bf16[16,1024]{1,0:T(8,128)(2,1)S(1)}, u32[]{:S(2)}, u32[]{:S(2)}) collective-permute-start(bf16[16,1024]{1,0:T(8,128)(2,1)S(1)} %get-tuple-element.34), channel_id=1, source_target_pairs={{0,32},{32,0},{64,96},{96,64},{1,33},{33,1},{65,97},{97,65},{2,34}... | collective-permute-start | bytes 98312 | tf_op jit(solution)/shard_map/ppermute | solution.py:368
  199.7 14.3 %collective-permute-start.12 = (bf16[8,1024]{1,0:T(8,128)(2,1)S(1)}, bf16[8,1024]{1,0:T(8,128)(2,1)S(1)}, u32[]{:S(2)}, u32[]{:S(2)}) collective-permute-start(bf16[8,1024]{1,0:T(8,128)(2,1)S(1)} %fusion), channel_id=1, source_target_pairs={{0,96},{32,64},{64,32},{96,0},{1,97},{33,65},{65,33},{97,1},{2,98}... | collective-permute-start | bytes 49160 | tf_op jit(solution)/shard_map/ppermute | solution.py:371

commit v4 on v3

--- a/solution.py
+++ b/solution.py
@@ -139,9 +139,10 @@
         window = slice(left, (tile + 1) * HD)
         rows, cols = iotas(HD, here.stop - left)
         rows, cols = rows + here.start, cols + left
-        first = jnp.zeros_like(rows)
+        first = jnp.zeros((HD, HD), jnp.int32)
         for start in starts[1:]:
-            first = jnp.where(rows >= start, start, first)
+            first = jnp.where(rows[:, :HD] >= start, start, first)
+        first = jnp.concatenate([first] * (rows.shape[1] // HD), axis=1)
         bias = jnp.where((cols <= rows) & (cols >= first), 0.0, NEG)
         bias = jnp.concatenate([bias] * GROUP, axis=0)
         probs = softmax(by_head(query_ref[here, :]), key_ref[window, :], bias)
@@ -314,31 +315,38 @@
     return lax.ppermute(value, axis, [(i, (i + step) % n) for i in range(n)])
 
 
-def pieces_kernel(choose, me_ref, own_ref, *refs):
-    *others, total_ref = refs
+def pieces_kernel(choose, columns, me_ref, own_ref, *refs):
+    *others, total_ref, turned_ref = refs
     total = own_ref[...]
     picks = choose(me_ref[0])
     for came in others[: len(others) - len(picks)]:
         total = total + came[...].astype(jnp.float32)
     total_ref[...] = total
+    if columns:
+        for b in range(total.shape[1] // HD):
+            at = pl.multiple_of(me_ref[1 + b] * HD, HD)
+            turned_ref[:, b * HD : (b + 1) * HD] = total_ref[:, pl.ds(at, HD)]
+        total_ref = turned_ref
     for out_ref, blocks in zip(others[len(others) - len(picks) :], picks):
         size = out_ref.shape[0] // len(blocks)
         parts = [total_ref[pl.ds(pl.multiple_of(b * size, 8), size), :] for b in blocks]
         out_ref[...] = jnp.concatenate(parts, axis=0).astype(out_ref.dtype)
 
 
-def pieces(axis, own, came, choose, shares):
+def pieces(axis, own, came, choose, shares, columns=None):
     me = lax.axis_index(axis).astype(jnp.int32).reshape(1)
+    if columns is not None:
+        me = jnp.concatenate([me, columns])
     rows, width = own.shape
     vmem = pl.BlockSpec(memory_space=pltpu.VMEM)
     return pl.pallas_call(
-        functools.partial(pieces_kernel, choose),
+        functools.partial(pieces_kernel, choose, columns is not None),
         out_shape=tuple(
             jax.ShapeDtypeStruct((rows * of // total, width), dtype) for of, total, dtype in shares
         ),
         in_specs=[pl.BlockSpec(memory_space=pltpu.SMEM)] + [vmem] * (1 + len(came)),
         out_specs=(vmem,) * len(shares),
-        scratch_shapes=[pltpu.VMEM((rows, width), jnp.float32)],
+        scratch_shapes=[pltpu.VMEM((rows, width), jnp.float32)] * 2,
         compiler_params=pltpu.CompilerParams(vmem_limit_bytes=24 << 20),
         name="pieces",
     )(me, own, *came)
@@ -358,13 +366,13 @@
     return own, got
 
 
-def exchange_far(axis, own, came):
+def exchange_far(axis, own, came, columns):
     def choose(me):
         first = jnp.bitwise_xor(me, 1)
         return [[first, 3 - first], [me], [3 - me]]
 
     shares = [(2, 4, LOW), (1, 4, jnp.float32), (1, 4, jnp.float32)]
-    away, mine, other = pieces(axis, own, came, choose, shares)
+    away, mine, other = pieces(axis, own, came, choose, shares, columns)
     got = lax.ppermute(away, axis, [(i, i ^ 1) for i in range(4)]).astype(jnp.float32)
     size = mine.shape[0]
     back = (other + got[size:]).astype(LOW)
@@ -389,12 +397,10 @@
     came = shift(away, "core", 1)
     own_sum, got = exchange("y", kept, [came], 1)
     own_sum, got = exchange("x", own_sum, got, lax.axis_size("zhi"))
-    total = exchange_far("zhi", own_sum, got)
-    total = total.reshape(-1, 2 * near, HD)
     zq, zr = lax.axis_index("zq"), lax.axis_index("zr")
-    block = jnp.arange(2 * near)
+    block = jnp.arange(2 * near, dtype=jnp.int32)
     source = 2 * jnp.bitwise_and(zr - block, near - 1) + (block // near != zq)
-    total = jnp.take(total, source, axis=1).reshape(total.shape[0], -1)
+    total = exchange_far("zhi", own_sum, got, source.astype(jnp.int32))
     query_grad, key_grad, value_grad = finish(received, packed.shape[0] // doc_plan.shape[1])
     return (query_grad[None], key_grad[None], value_grad[None], total)
 

time: 219 us -> 219 us (level)
  no operation moved by 1% of the time
where the time goes in v4:
time: 219 us; the launch traced here: 218 us
  waiting for transfers between devices  97.7 us (45%)
  starting transfers between devices  94.7 us (43%)
  Pallas kernels  20.3 us (9%)
  local copies, waits for them, and re-layouts  2.87 us (1%)
    ppermute x11, waiting for transfers between devices, shift(): return lax.ppermute(value, axis, [(i, (i + step) % n) for i in range(n)])  92.4 us
    ppermute x11, starting transfers between devices, shift(): return lax.ppermute(value, axis, [(i, (i + step) % n) for i in range(n)])  39.9 us
    all_to_all x1, starting transfers between devices, shards(): lax.all_to_all(packed, ('zhi', 'x'), split_axis=0, concat_axis=0, tiled=T...  30.4 us
    ppermute x1, starting transfers between devices, exchange_far(): lax.ppermute(away, axis, [(i, i ^ 1) for i in range(4)]).astype(jnp.float32)  13.4 us
    pallas_call x2, Pallas kernels, local_call(): pl.pallas_call(kernel, out_shape=out_shape(packed), in_specs=[smem] * 3 +...  12.4 us
    ppermute x1, starting transfers between devices, exchange_far(): back = lax.ppermute(back, axis, [(i, 3 - i) for i in range(4)])  10.9 us
  transfers between devices with their start and end apart: 14, of which 11 were waited for; matrix products, arithmetic and copies ran while one was open for 1% of the time, Pallas kernels for 4%

profile of v4, /device:TPU:46, one launch (start us, length us, event | category | flops | bytes accessed | tf_op | source)
XLA Modules:
  0.0 218.0 jit_solution(2998209532221708160)
XLA Ops:
  0.6 7.8 %shard_map.102 = bf16[640,512]{1,0:T(8,128)(2,1)} custom-call(s32[1]{0:T(128)} %bitcast.index_ref, s32[16,16]{1,0:T(8,128)} %lengths_ref.3, s32[16,16]{1,0:T(8,128)} %plan_ref.3, bf16[512,512]{1,0:T(8,128)(2,1)} %bitcast.19, bf16[512,128]{1,0:T(8,128)(2,1)} %bitcast.26, bf16[512,128]{1,0:T(8,128)(2,1)} %bitcast.25, bf16[512,512]{1,0:T(8,128)(2,1)} %bitcast.21), custom_call_target="tpu_custom_call" | custom-call | flops 2000000000 | bytes 1310720 | tf_op jit(solution)/shard_map/pallas_call | solution.py:215
  8.5 30.4 %all-to-all-start = ((bf16[16,40,512]{2,1,0:T(8,128)(2,1)}), bf16[16,40,512]{2,1,0:T(8,128)(2,1)S(1)}, u32[]{:S(2)}, u32[]{:S(2)}) async-start(bf16[16,40,512]{2,1,0:T(8,128)(2,1)} %bitcast.17), calls=%async_computation | async-start | bytes 1310720 | tf_op jit(solution)/shard_map/all_to_all | solution.py:394
  38.9 4.6 %shard_map.103 = bf16[512,128]{1,0:T(8,128)(2,1)} custom-call(s32[1]{0:T(128)} %bitcast.index_ref, s32[16,16]{1,0:T(8,128)} %lengths_ref.3, s32[16,16]{1,0:T(8,128)} %plan_ref.3, bf16[512,512]{1,0:T(8,128)(2,1)} %bitcast.20, bf16[512,128]{1,0:T(8,128)(2,1)} %bitcast.27, bf16[512,512]{1,0:T(8,128)(2,1)} %bitcast.22), custom_call_target="tpu_custom_call" | custom-call | flops 1000000000 | bytes 1179648 | tf_op jit(solution)/shard_map/pallas_call | solution.py:215
  43.5 4.3 %collective-permute-start = (bf16[512,128]{1,0:T(8,128)(2,1)}, bf16[512,128]{1,0:T(8,128)(2,1)S(1)}, u32[]{:S(2)}, u32[]{:S(2)}) collective-permute-start(bf16[512,128]{1,0:T(8,128)(2,1)} %shard_map.103), channel_id=1, source_target_pairs={{0,4},{4,0},{1,5},{5,1},{2,6},{6,2},{3,7},{7,3},{8,12},{12,8},{9,1... | collective-permute-start | bytes 393224 | tf_op jit(solution)/shard_map/ppermute | solution.py:315
  47.8 56.3 %collective-permute-done = bf16[512,128]{1,0:T(8,128)(2,1)S(1)} collective-permute-done((bf16[512,128]{1,0:T(8,128)(2,1)}, bf16[512,128]{1,0:T(8,128)(2,1)S(1)}, u32[]{:S(2)}, u32[]{:S(2)}) %collective-permute-start) | collective-permute-done | bytes 131104 | tf_op jit(solution)/shard_map/ppermute | solution.py:315
  106.9 10.0 %collective-permute-start.2 = (bf16[512,256]{1,0:T(8,128)(2,1)S(1)}, bf16[512,256]{1,0:T(8,128)(2,1)S(1)}, u32[]{:S(2)}, u32[]{:S(2)}) collective-permute-start(bf16[512,256]{1,0:T(8,128)(2,1)S(1)} %pad_maximum_fusion.refs_0_), channel_id=1, source_target_pairs={{0,2},{1,3},{2,0},{3,1},{4,6},{5,7},{6,4},{7,5},{8,10},{9,11},{10,... | collective-permute-start | bytes 786440 | tf_op jit(solution)/shard_map/ppermute | solution.py:315
  120.3 12.0 %collective-permute-done.2.refs_2_ = bf16[512,256]{1,0:T(8,128)(2,1)S(1)} collective-permute-done((bf16[512,256]{1,0:T(8,128)(2,1)S(1)}, bf16[512,256]{1,0:T(8,128)(2,1)S(1)}, u32[]{:S(2)}, u32[]{:S(2)}) %collective-permute-start.2) | collective-permute-done | bytes 262176 | tf_op jit(solution)/shard_map/ppermute | solution.py:315
  132.3 4.2 %collective-permute-done.3.refs_3_ = bf16[512,256]{1,0:T(8,128)(2,1)S(1)} collective-permute-done((bf16[512,256]{1,0:T(8,128)(2,1)S(1)}, bf16[512,256]{1,0:T(8,128)(2,1)S(1)}, u32[]{:S(2)}, u32[]{:S(2)}) %collective-permute-start.3) | collective-permute-done | bytes 262176 | tf_op jit(solution)/shard_map/ppermute | solution.py:315
  141.3 1.9 collective-permute-start.4
  143.2 2.9 %collective-permute-done.4.refs_0_ = bf16[512,1024]{1,0:T(8,128)(2,1)} collective-permute-done((bf16[512,1024]{1,0:T(8,128)(2,1)}, bf16[512,1024]{1,0:T(8,128)(2,1)}, u32[]{:S(2)}, u32[]{:S(2)}) %collective-permute-start.4) | collective-permute-done | bytes 1048608 | tf_op jit(solution)/shard_map/ppermute | solution.py:315
  146.2 2.4 %pieces.3 = (f32[128,1024]{1,0:T(8,128)S(1)}, bf16[128,1024]{1,0:T(8,128)(2,1)}, bf16[128,1024]{1,0:T(8,128)(2,1)}, bf16[128,1024]{1,0:T(8,128)(2,1)S(1)}) custom-call(s32[1]{0:T(128)} %bitcast.12.me_ref, f32[512,1024]{1,0:T(8,128)S(1)} %get-tuple-element.23.own_ref, bf16[512,1024]{1,0:T(8,128)(2,1)} %collective-permute-done.4.refs_0_), custom_call_target="tpu_custom_call" | custom-call | tf_op jit(solution)/shard_map/pieces/pallas_call | solution.py:342
  148.6 3.5 %collective-permute-start.5 = (bf16[128,1024]{1,0:T(8,128)(2,1)}, bf16[128,1024]{1,0:T(8,128)(2,1)S(1)}, u32[]{:S(2)}, u32[]{:S(2)}) collective-permute-start(bf16[128,1024]{1,0:T(8,128)(2,1)} %get-tuple-element.26), channel_id=1, source_target_pairs={{0,256},{256,512},{512,768},{768,0},{1,257},{257,513},{513,769},{7... | collective-permute-start | bytes 786440 | tf_op jit(solution)/shard_map/ppermute | solution.py:315
  152.0 2.9 %collective-permute-start.6 = (bf16[128,1024]{1,0:T(8,128)(2,1)}, bf16[128,1024]{1,0:T(8,128)(2,1)S(1)}, u32[]{:S(2)}, u32[]{:S(2)}) collective-permute-start(bf16[128,1024]{1,0:T(8,128)(2,1)} %get-tuple-element.27), channel_id=1, source_target_pairs={{0,512},{256,768},{512,0},{768,256},{1,513},{257,769},{513,1},{769... | collective-permute-start | bytes 786440 | tf_op jit(solution)/shard_map/ppermute | solution.py:315
  154.9 4.3 %collective-permute-start.7 = (bf16[128,1024]{1,0:T(8,128)(2,1)S(1)}, bf16[128,1024]{1,0:T(8,128)(2,1)S(1)}, u32[]{:S(2)}, u32[]{:S(2)}) collective-permute-start(bf16[128,1024]{1,0:T(8,128)(2,1)S(1)} %get-tuple-element.28), channel_id=1, source_target_pairs={{0,768},{256,0},{512,256},{768,512},{1,769},{257,1},{513,257},{769... | collective-permute-start | bytes 786440 | tf_op jit(solution)/shard_map/ppermute | solution.py:315
  159.8 5.0 %collective-permute-done.6.refs_1_ = bf16[128,1024]{1,0:T(8,128)(2,1)S(1)} collective-permute-done((bf16[128,1024]{1,0:T(8,128)(2,1)}, bf16[128,1024]{1,0:T(8,128)(2,1)S(1)}, u32[]{:S(2)}, u32[]{:S(2)}) %collective-permute-start.6) | collective-permute-done | bytes 262176 | tf_op jit(solution)/shard_map/ppermute | solution.py:315
  164.9 4.5 %collective-permute-done.7.refs_2_ = bf16[128,1024]{1,0:T(8,128)(2,1)S(1)} collective-permute-done((bf16[128,1024]{1,0:T(8,128)(2,1)S(1)}, bf16[128,1024]{1,0:T(8,128)(2,1)S(1)}, u32[]{:S(2)}, u32[]{:S(2)}) %collective-permute-start.7) | collective-permute-done | bytes 262176 | tf_op jit(solution)/shard_map/ppermute | solution.py:315
  169.5 2.8 %collective-permute-start.10 = (bf16[32,1024]{1,0:T(8,128)(2,1)S(1)}, bf16[32,1024]{1,0:T(8,128)(2,1)S(1)}, u32[]{:S(2)}, u32[]{:S(2)}) collective-permute-start(bf16[32,1024]{1,0:T(8,128)(2,1)S(1)} %get-tuple-element.32), channel_id=1, source_target_pairs={{0,24},{8,0},{16,8},{24,16},{1,25},{9,1},{17,9},{25,17},{2,26},{10... | collective-permute-start | bytes 196616 | tf_op jit(solution)/shard_map/ppermute | solution.py:315
  172.3 4.3 %collective-permute-start.8 = (bf16[32,1024]{1,0:T(8,128)(2,1)S(1)}, bf16[32,1024]{1,0:T(8,128)(2,1)S(1)}, u32[]{:S(2)}, u32[]{:S(2)}) collective-permute-start(bf16[32,1024]{1,0:T(8,128)(2,1)S(1)} %get-tuple-element.30), channel_id=1, source_target_pairs={{0,8},{8,16},{16,24},{24,0},{1,9},{9,17},{17,25},{25,1},{2,10},{10... | collective-permute-start | bytes 196616 | tf_op jit(solution)/shard_map/ppermute | solution.py:315
  176.6 2.2 collective-permute-start.9
  178.9 5.4 %collective-permute-done.9.refs_1_ = bf16[32,1024]{1,0:T(8,128)(2,1)S(1)} collective-permute-done((bf16[32,1024]{1,0:T(8,128)(2,1)S(1)}, bf16[32,1024]{1,0:T(8,128)(2,1)S(1)}, u32[]{:S(2)}, u32[]{:S(2)}) %collective-permute-start.9) | collective-permute-done | bytes 65568 | tf_op jit(solution)/shard_map/ppermute | solution.py:315
  184.9 13.4 %collective-permute-start.11 = (bf16[16,1024]{1,0:T(8,128)(2,1)S(1)}, bf16[16,1024]{1,0:T(8,128)(2,1)S(1)}, u32[]{:S(2)}, u32[]{:S(2)}) collective-permute-start(bf16[16,1024]{1,0:T(8,128)(2,1)S(1)} %get-tuple-element.34), channel_id=1, source_target_pairs={{0,32},{32,0},{64,96},{96,64},{1,33},{33,1},{65,97},{97,65},{2,34}... | collective-permute-start | bytes 98312 | tf_op jit(solution)/shard_map/ppermute | solution.py:376
  200.2 10.9 %collective-permute-start.12 = (bf16[8,1024]{1,0:T(8,128)(2,1)S(1)}, bf16[8,1024]{1,0:T(8,128)(2,1)S(1)}, u32[]{:S(2)}, u32[]{:S(2)}) collective-permute-start(bf16[8,1024]{1,0:T(8,128)(2,1)S(1)} %fusion), channel_id=1, source_target_pairs={{0,96},{32,64},{64,32},{96,0},{1,97},{33,65},{65,33},{97,1},{2,98}... | collective-permute-start | bytes 49160 | tf_op jit(solution)/shard_map/ppermute | solution.py:379
  211.1 3.4 %collective-permute-done.12 = bf16[8,1024]{1,0:T(8,128)(2,1)S(1)} collective-permute-done((bf16[8,1024]{1,0:T(8,128)(2,1)S(1)}, bf16[8,1024]{1,0:T(8,128)(2,1)S(1)}, u32[]{:S(2)}, u32[]{:S(2)}) %collective-permute-start.12) | collective-permute-done | bytes 16416 | tf_op jit(solution)/shard_map/ppermute | solution.py:379
  215.2 2.7 %finish.1 = (bf16[640,512]{1,0:T(8,128)(2,1)}, bf16[640,128]{1,0:T(8,128)(2,1)}, bf16[640,128]{1,0:T(8,128)(2,1)}) custom-call(bf16[640,512]{1,0:T(8,128)(2,1)S(1)} %bitcast.15), custom_call_target="tpu_custom_call" | custom-call | tf_op jit(solution)/shard_map/finish/pallas_call | solution.py:272
  (23 shorter events, 14.9 us)
Async XLA Ops:
  8.5 206.7 %all-to-all-start = ((bf16[16,40,512]{2,1,0:T(8,128)(2,1)}), bf16[16,40,512]{2,1,0:T(8,128)(2,1)S(1)}, u32[]{:S(2)}, u32[]{:S(2)}) async-start(bf16[16,40,512]{2,1,0:T(8,128)(2,1)} %bitcast.17), calls=%async_computation | async-start | bytes 1310720 | tf_op jit(solution)/shard_map/all_to_all | solution.py:394
  43.5 60.6 %collective-permute-start = (bf16[512,128]{1,0:T(8,128)(2,1)}, bf16[512,128]{1,0:T(8,128)(2,1)S(1)}, u32[]{:S(2)}, u32[]{:S(2)}) collective-permute-start(bf16[512,128]{1,0:T(8,128)(2,1)} %shard_map.103), channel_id=1, source_target_pairs={{0,4},{4,0},{1,5},{5,1},{2,6},{6,2},{3,7},{7,3},{8,12},{12,8},{9,1... | collective-permute-start | bytes 393224 | tf_op jit(solution)/shard_map/ppermute | solution.py:315
  105.0 15.3 %collective-permute-start.1 = (bf16[512,256]{1,0:T(8,128)(2,1)S(1)}, bf16[512,256]{1,0:T(8,128)(2,1)S(1)}, u32[]{:S(2)}, u32[]{:S(2)}) collective-permute-start(bf16[512,256]{1,0:T(8,128)(2,1)S(1)} %pad_maximum_fusion.refs_0_), channel_id=1, source_target_pairs={{0,1},{1,2},{2,3},{3,0},{4,5},{5,6},{6,7},{7,4},{8,9},{9,10},{10,1... | collective-permute-start | bytes 786440 | tf_op jit(solution)/shard_map/ppermute | solution.py:315
  106.9 25.4 %collective-permute-start.2 = (bf16[512,256]{1,0:T(8,128)(2,1)S(1)}, bf16[512,256]{1,0:T(8,128)(2,1)S(1)}, u32[]{:S(2)}, u32[]{:S(2)}) collective-permute-start(bf16[512,256]{1,0:T(8,128)(2,1)S(1)} %pad_maximum_fusion.refs_0_), channel_id=1, source_target_pairs={{0,2},{1,3},{2,0},{3,1},{4,6},{5,7},{6,4},{7,5},{8,10},{9,11},{10,... | collective-permute-start | bytes 786440 | tf_op jit(solution)/shard_map/ppermute | solution.py:315
  116.9 19.6 %collective-permute-start.3 = (bf16[512,256]{1,0:T(8,128)(2,1)S(1)}, bf16[512,256]{1,0:T(8,128)(2,1)S(1)}, u32[]{:S(2)}, u32[]{:S(2)}) collective-permute-start(bf16[512,256]{1,0:T(8,128)(2,1)S(1)} %pad_maximum_fusion.refs_0_), channel_id=1, source_target_pairs={{0,3},{1,0},{2,1},{3,2},{4,7},{5,4},{6,5},{7,6},{8,11},{9,8},{10,9... | collective-permute-start | bytes 786440 | tf_op jit(solution)/shard_map/ppermute | solution.py:315
  136.5 0.7 copy-start.1
  137.2 1.2 copy-start
  138.5 0.9 copy-start.2
  141.3 4.9 %collective-permute-start.4 = (bf16[512,1024]{1,0:T(8,128)(2,1)}, bf16[512,1024]{1,0:T(8,128)(2,1)}, u32[]{:S(2)}, u32[]{:S(2)}) collective-permute-start(bf16[512,1024]{1,0:T(8,128)(2,1)} %get-tuple-element.24), channel_id=1, source_target_pairs={{0,128},{128,0},{1,129},{129,1},{2,130},{130,2},{3,131},{131,3},{4... | collective-permute-start | bytes 3145736 | tf_op jit(solution)/shard_map/ppermute | solution.py:315
  148.6 11.3 %collective-permute-start.5 = (bf16[128,1024]{1,0:T(8,128)(2,1)}, bf16[128,1024]{1,0:T(8,128)(2,1)S(1)}, u32[]{:S(2)}, u32[]{:S(2)}) collective-permute-start(bf16[128,1024]{1,0:T(8,128)(2,1)} %get-tuple-element.26), channel_id=1, source_target_pairs={{0,256},{256,512},{512,768},{768,0},{1,257},{257,513},{513,769},{7... | collective-permute-start | bytes 786440 | tf_op jit(solution)/shard_map/ppermute | solution.py:315
  152.0 12.8 %collective-permute-start.6 = (bf16[128,1024]{1,0:T(8,128)(2,1)}, bf16[128,1024]{1,0:T(8,128)(2,1)S(1)}, u32[]{:S(2)}, u32[]{:S(2)}) collective-permute-start(bf16[128,1024]{1,0:T(8,128)(2,1)} %get-tuple-element.27), channel_id=1, source_target_pairs={{0,512},{256,768},{512,0},{768,256},{1,513},{257,769},{513,1},{769... | collective-permute-start | bytes 786440 | tf_op jit(solution)/shard_map/ppermute | solution.py:315
  154.9 14.4 %collective-permute-start.7 = (bf16[128,1024]{1,0:T(8,128)(2,1)S(1)}, bf16[128,1024]{1,0:T(8,128)(2,1)S(1)}, u32[]{:S(2)}, u32[]{:S(2)}) collective-permute-start(bf16[128,1024]{1,0:T(8,128)(2,1)S(1)} %get-tuple-element.28), channel_id=1, source_target_pairs={{0,768},{256,0},{512,256},{768,512},{1,769},{257,1},{513,257},{769... | collective-permute-start | bytes 786440 | tf_op jit(solution)/shard_map/ppermute | solution.py:315
  169.5 9.3 %collective-permute-start.10 = (bf16[32,1024]{1,0:T(8,128)(2,1)S(1)}, bf16[32,1024]{1,0:T(8,128)(2,1)S(1)}, u32[]{:S(2)}, u32[]{:S(2)}) collective-permute-start(bf16[32,1024]{1,0:T(8,128)(2,1)S(1)} %get-tuple-element.32), channel_id=1, source_target_pairs={{0,24},{8,0},{16,8},{24,16},{1,25},{9,1},{17,9},{25,17},{2,26},{10... | collective-permute-start | bytes 196616 | tf_op jit(solution)/shard_map/ppermute | solution.py:315
  172.3 6.5 %collective-permute-start.8 = (bf16[32,1024]{1,0:T(8,128)(2,1)S(1)}, bf16[32,1024]{1,0:T(8,128)(2,1)S(1)}, u32[]{:S(2)}, u32[]{:S(2)}) collective-permute-start(bf16[32,1024]{1,0:T(8,128)(2,1)S(1)} %get-tuple-element.30), channel_id=1, source_target_pairs={{0,8},{8,16},{16,24},{24,0},{1,9},{9,17},{17,25},{25,1},{2,10},{10... | collective-permute-start | bytes 196616 | tf_op jit(solution)/shard_map/ppermute | solution.py:315
  176.6 7.7 %collective-permute-start.9 = (bf16[32,1024]{1,0:T(8,128)(2,1)S(1)}, bf16[32,1024]{1,0:T(8,128)(2,1)S(1)}, u32[]{:S(2)}, u32[]{:S(2)}) collective-permute-start(bf16[32,1024]{1,0:T(8,128)(2,1)S(1)} %get-tuple-element.31), channel_id=1, source_target_pairs={{0,16},{8,24},{16,0},{24,8},{1,17},{9,25},{17,1},{25,9},{2,18},{10... | collective-permute-start | bytes 196616 | tf_op jit(solution)/shard_map/ppermute | solution.py:315
  184.9 15.3 %collective-permute-start.11 = (bf16[16,1024]{1,0:T(8,128)(2,1)S(1)}, bf16[16,1024]{1,0:T(8,128)(2,1)S(1)}, u32[]{:S(2)}, u32[]{:S(2)}) collective-permute-start(bf16[16,1024]{1,0:T(8,128)(2,1)S(1)} %get-tuple-element.34), channel_id=1, source_target_pairs={{0,32},{32,0},{64,96},{96,64},{1,33},{33,1},{65,97},{97,65},{2,34}... | collective-permute-start | bytes 98312 | tf_op jit(solution)/shard_map/ppermute | solution.py:376
  200.2 14.3 %collective-permute-start.12 = (bf16[8,1024]{1,0:T(8,128)(2,1)S(1)}, bf16[8,1024]{1,0:T(8,128)(2,1)S(1)}, u32[]{:S(2)}, u32[]{:S(2)}) collective-permute-start(bf16[8,1024]{1,0:T(8,128)(2,1)S(1)} %fusion), channel_id=1, source_target_pairs={{0,96},{32,64},{64,32},{96,0},{1,97},{33,65},{65,33},{97,1},{2,98}... | collective-permute-start | bytes 49160 | tf_op jit(solution)/shard_map/ppermute | solution.py:379
